TPU v7x, 32 devices: a whole 2x2x4 slice. The times are simulated.
32 devices in a mesh: proj: 4 (over x, core), scen: 8 (over z, y).
Axes of the slice: x: 2, y: 2, z: 4, core: 2. Of those that a mesh axis runs over, the one named last changes fastest.
Arguments:
- fund_value: float32 [4096, 1024], P('proj', 'scen'), may hold values from 0.5 to 2
- in_force: float32 [4096, 1024], P('proj', 'scen'), may hold values from 0.5 to 1.5
- guarantee_base: float32 [4096, 1024], P('proj', 'scen'), may hold values from 0.5 to 2
- lapse_rate: float32 [4096, 1024], P('proj', 'scen'), may hold values from 0.02 to 0.4
- cohort: int32 [4096], P('proj'), may hold values from 0 to 511, as said below
- product: int32 [4096], P('proj'), may hold values from 0 to 15
- guarantee_type: int32 [4096], P('proj'), may hold values from 0 to 3
- returns: float32 [8, 12, 1024], P(None, None, 'scen'), may hold values from -0.625 to 0.625
- mix_table: float32 [16, 8], replicated, may hold values from 0.05 to 1
- fee_table: float32 [4], replicated, may hold values from 0.001 to 0.01
- rollup_table: float32 [4], replicated, may hold values from 0.01 to 0.08
- fund_vol: float32 [8], replicated, may hold values from 0.15 to 0.6
- closing_sigma_figure: float32 [1024], P('scen'), may hold values from 0.5 to 2
- shocks: float32 [8, 2, 1024], P(None, None, 'scen'), may hold values from -6 to 6
- base_table: float32 [10, 16], replicated, may hold values from 0.03 to 0.2
- year_index: int32 [1], replicated, may hold values from 0 to 9
Outputs:
- fund_next: float32 [4096, 1024], P('proj', 'scen')
- force_next: float32 [4096, 1024], P('proj', 'scen')
- base_next: float32 [4096, 1024], P('proj', 'scen')
- lapse_next: float32 [4096, 1024], P('proj', 'scen')
- benefit_cost_per_account: float32 [512, 1024], P('proj', 'scen')
Inputs may be any that keep to these rules, and one draw needn't show every extreme that they name: Each cohort holds exactly 8 model points; the model points of each index of proj include exactly 256 whose cohorts lie in the block of 128 cohorts that any one index of proj owns (cohorts q * 128 onward for index q).
All inputs are finite; a program needn't handle non-finite values.
Results may differ from a plain program's by a relative error of at most 0.00026.
Values sent between devices are 32-bit elements; how exact they have to be, the bound alone decides.
No kernel may reach another device: no remote copies, remote signals or barrier semaphores. Data moves between devices by JAX's collectives and lax.ppermute only.
A program may use at most 64 MiB of HBM per device.

v0:
```python
import functools
import math

import jax
import jax.numpy as jnp
from jax import lax
from jax.experimental import pallas as pl
from jax.experimental.pallas import tpu as pltpu
from jax.sharding import PartitionSpec as P


COHORTS = 512
MONTHS_PER_YEAR = 12.0
DISCOUNT = 0.96
LAPSE_FLOOR, LAPSE_SPAN, LAPSE_SLOPE, LAPSE_PIVOT = 0.3, 2.0, 5.0, 0.4
LOG2E = 1.0 / math.log(2.0)
LANES = 128
DEPTH = 64
HIGHEST = lax.Precision.HIGHEST
F32, BF16, I32 = jnp.float32, jnp.bfloat16, jnp.int32
VMEM = pl.BlockSpec(memory_space=pltpu.VMEM)
SMEM = pl.BlockSpec(memory_space=pltpu.SMEM)
HBM = pl.BlockSpec(memory_space=pltpu.HBM)


def dot(a, b):
    return jnp.dot(a, b, preferred_element_type=F32)


def iota(shape, axis):
    return lax.broadcasted_iota(I32, shape, axis)


def split(x, parts):
    out = []
    for _ in range(parts):
        top = x.astype(BF16).astype(F32)
        out.append(top)
        x = x - top
    return out


def halves(x):
    return jnp.concatenate(split(x, 2), axis=1).astype(BF16)


def join(x):
    return x[:, :LANES] + x[:, LANES:]


def onehot(row, shape):
    return (iota(shape, 0) == row).astype(BF16)


def vmem(x):
    return pltpu.with_memory_space_constraint(x, pltpu.VMEM)


def hbm(x):
    return pltpu.with_memory_space_constraint(x, pltpu.HBM)


def limit(mebibytes):
    return pltpu.CompilerParams(vmem_limit_bytes=mebibytes << 20)


def relabel(cohort, owned, me):
    shift = owned.bit_length() - 1
    owner = jnp.bitwise_xor(lax.shift_right_logical(cohort, shift), me)
    return owner, lax.shift_left(owner, shift) + jnp.bitwise_and(cohort, owned - 1)


def project_kernel(dims, me_ref, year_ref, fee_ref, roll_ref, cohort_ref, product_ref, type_ref, mix_ref, base_ref,
                   returns_ref, fund_hbm, force_hbm, guar_hbm, lapse_hbm, *rest):
    n_proj, owned, rows, months, products, types = dims
    sends = rest[:n_proj]
    (level_ref, fund_out, force_out, guar_out, fund, force, guar, lapse, grow, table, hot, weighted, secured,
     move, gather, in_sem, out_sem) = rest[n_proj:]
    points = fund.shape[0]
    blocks = points // LANES
    combos = products * types
    sources = ((fund_hbm, fund), (guar_hbm, guar), (lapse_hbm, lapse), (force_hbm, force))
    sinks = ((fund, fund_out), (guar, guar_out), (force, force_out))

    def fetch(a):
        return pltpu.make_async_copy(*sources[a], in_sem.at[a])

    def flush(a):
        return pltpu.make_async_copy(*sinks[a], out_sem.at[a])

    for a in range(4):
        fetch(a).start()

    combo_product = lax.shift_right_logical(iota((combos, products), 0), types.bit_length() - 1)
    pick = (combo_product == iota((combos, products), 1)).astype(F32)
    mix = mix_ref[...].T
    mix = mix / jnp.sum(mix, axis=1, keepdims=True)
    mix = jnp.dot(pick, mix, precision=HIGHEST, preferred_element_type=F32)
    combo_type = jnp.bitwise_and(iota((combos, LANES), 0), types - 1)
    fee = jnp.zeros((combos, LANES), F32)
    roll = jnp.zeros((combos, LANES), F32)
    for g in range(types):
        fee = jnp.where(combo_type == g, fee_ref[g], fee)
        roll = jnp.where(combo_type == g, roll_ref[g], roll)
    keep = 1.0 - fee

    def put(column, value):
        for i, part in enumerate(split(value, 3)):
            table[i * combos:(i + 1) * combos, column * LANES:(column + 1) * LANES] = part.astype(BF16)

    for t in range(months):
        growth = 1.0 + jnp.dot(mix, returns_ref[t], precision=HIGHEST, preferred_element_type=F32)
        put(t, growth * keep)
    put(months, 1.0 + roll / MONTHS_PER_YEAR)
    level = jnp.sum(pick * base_ref[pl.ds(year_ref[0], 1), :], axis=1, keepdims=True)
    put(months + 1, jnp.broadcast_to(level, (combos, LANES)))

    combo = (product_ref[...] * types + type_ref[...]).astype(F32).T
    slot = jnp.bitwise_and(iota((LANES, 3 * combos), 1), combos - 1).astype(F32)
    for b in range(blocks):
        column = jnp.broadcast_to(combo[:, b:b + 1], (LANES, 3 * combos))
        hot[b * LANES:(b + 1) * LANES, :] = (column == slot).astype(BF16)

    owner = relabel(cohort_ref[...], owned, me_ref[0])[0]
    masks = jnp.concatenate([(owner == q).astype(F32) for q in range(n_proj)], axis=0)
    lower = (iota((LANES, LANES), 0) < iota((LANES, LANES), 1)).astype(BF16)
    before = dot(masks.astype(BF16), lower)
    count = dot(masks.astype(BF16), jnp.ones((LANES, LANES), BF16))
    size = n_proj * blocks
    r, c = iota((size, size), 0), iota((size, size), 1)
    shift = blocks.bit_length() - 1
    ahead = (lax.shift_right_logical(r, shift) == lax.shift_right_logical(c, shift)) & (c < r)
    before = before + dot(ahead.astype(BF16), count.astype(BF16))
    place = jnp.zeros((blocks, LANES), F32)
    for q in range(n_proj):
        span = slice(q * blocks, (q + 1) * blocks)
        place = place + masks[span] * before[span]

    local = jnp.bitwise_and(cohort_ref[...], owned - 1)
    place = place.astype(I32)
    kind = product_ref[...].astype(F32)
    which = iota((16, LANES), 0)
    facts = jnp.concatenate(
        [jnp.where(which == 0, kind[b:b + 1], jnp.where(which == 1, local[b:b + 1].astype(F32), 0.0)) for b in range(blocks)],
        axis=1).astype(BF16)
    for o in range(n_proj):
        mine = owner == o
        rank = jnp.where(mine, place, -1)
        label = jnp.where(mine, local, -1)
        for b in range(blocks):
            span = slice(b * LANES, (b + 1) * LANES)
            move[o * rows:(o + 1) * rows, span] = onehot(rank[b:b + 1], (rows, LANES))
            gather[o * owned:(o + 1) * owned, span] = onehot(label[b:b + 1], (owned, LANES))
    tail = dot(hot[...], table[:, months * LANES:])
    grow[...] = tail[:, :LANES]
    level_ref[...] = tail[:, LANES:]
    for a in range(2):
        fetch(a).wait()
    for t in range(0, months, 2):
        factors = dot(hot[...], table[:, t * LANES:(t + 2) * LANES])
        f = fund[...] * factors[:, :LANES]
        g = jnp.maximum(guar[...] * grow[...], f)
        f = f * factors[:, LANES:]
        guar[...] = jnp.maximum(g * grow[...], f)
        fund[...] = f
    flush(0).start()
    flush(1).start()
    for a in range(2, 4):
        fetch(a).wait()
    stay = 1.0 - lapse[...] / MONTHS_PER_YEAR
    stay = stay * stay * stay
    stay = stay * stay
    n = force[...] * (stay * stay)
    force[...] = n
    flush(2).start()
    weighted[...] = halves(n * fund[...])
    secured[...] = halves(n * guar[...])

    moved = join(dot(move[...], weighted[...]))
    summed = join(dot(gather[...], secured[...]))
    told = lax.dot_general(facts, move[...], (((1,), (1,)), ((), ())), preferred_element_type=F32)
    for o in range(n_proj):
        send = sends[o]
        send[:rows, :] = moved[o * rows:(o + 1) * rows]
        send[rows:rows + owned, :] = summed[o * owned:(o + 1) * owned]
        for b in range(rows // LANES):
            start = rows + owned + 8 * b
            first = o * rows + b * LANES
            send[start:start + 8, :] = told[:8, first:first + LANES]

    for a in range(3):
        flush(a).wait()


def hot_kernel(owned, me_ref, cohort_ref, hot_ref):
    _, label = relabel(cohort_ref[...], owned, me_ref[0])
    label = label.astype(F32).T
    slot = iota((LANES, hot_ref.shape[1]), 1).astype(F32)
    for b in range(hot_ref.shape[0] // LANES):
        column = jnp.broadcast_to(label[:, b:b + 1], slot.shape)
        hot_ref[b * LANES:(b + 1) * LANES, :] = (column == slot).astype(BF16)


def paths_kernel(shocks_ref, paths_ref):
    sources, funds, horizon, width = shocks_ref.shape
    count = sources * width
    which = iota((2 * funds, width), 0)
    for b in range(sources):
        total = jnp.zeros((funds, width), F32)
        for h in range(horizon):
            total = total + shocks_ref[b, :, h, :]
            p1, p2, p3 = split(total, 3)
            ones = jnp.where(which < 3, float(h + 1), jnp.where(which < 6, 1.0, 0.0))
            full = jnp.concatenate([p1, p1, p2, p2, p3, p1, ones], axis=0)
            start = h * count + b * width
            paths_ref[start:start + width, :] = full.T.astype(BF16)


def value_kernel(dims, vol_ref, sigma_ref, mix_ref, paths_ref, *rest):
    n_proj, owned, rows, horizon, group, step = dims
    received = rest[:n_proj]
    cost_ref, weighted, mixes, loads, spare, money = rest[n_proj:]
    funds, products = mix_ref.shape
    trials = paths_ref.shape[0] // horizon
    per = rows // LANES
    mix = mix_ref[...]
    mix = mix / jnp.sum(mix, axis=0, keepdims=True)
    tops, lows = [], []
    labels = []
    for o in range(n_proj):
        weighted[o * rows:(o + 1) * rows, :] = halves(received[o][:rows, :])
        for b in range(per):
            start = rows + owned + 8 * b
            facts = received[o][start:start + 8, :]
            hot = (jnp.broadcast_to(facts[0:1], (products, LANES)).astype(I32) == iota((products, LANES), 0)).astype(F32)
            share = lax.dot_general(mix, hot, (((1,), (0,)), ((), ())), precision=HIGHEST, preferred_element_type=F32)
            top, low = split(share, 2)
            tops.append(top)
            lows.append(low)
            labels.append(facts[1:2].astype(I32))
    spans = n_proj * per
    for b in range(spans):
        mixes[0, b] = tops[b]
        mixes[1, b] = lows[b]
    vol = jnp.zeros((funds, LANES), F32)
    for f in range(funds):
        vol = jnp.where(iota((funds, LANES), 0) == f, vol_ref[f], vol)
    sigma = sigma_ref[...]
    scale = sigma * LOG2E
    slope = -0.5 * sigma * sigma * LOG2E
    which = iota((funds, LANES), 0)

    def prepare(i, loads):
        first = i * group
        sides = []
        for part in range(2):
            wide = []
            for b in range(spans):
                share = mixes[part, b]
                wide.append(jnp.concatenate(
                    [jnp.where(labels[b] == first + c, share, 0.0) for c in range(group)], axis=0).astype(BF16))
            sides.append(jnp.concatenate(wide, axis=1))
        sums = join(dot(sides[0], weighted[...]) + dot(sides[1], weighted[...]))
        span = pl.ds(pl.multiple_of(rows + first, 8), group)
        secured = received[0][span, :]
        for o in range(1, n_proj):
            secured = secured + received[o][span, :]
        for c in range(group):
            part = sums[c * funds:(c + 1) * funds]
            inverse = 1.0 / jnp.sum(part, axis=0, keepdims=True)
            load = part * inverse * vol
            ratio = secured[c:c + 1] * inverse
            money[pl.ds(first + c, 1), :] = ratio
            spread = jnp.sum(load * load, axis=0, keepdims=True)
            w1, w2, w3 = split(load * scale, 3)
            d = split(slope * spread, 3) + split(-LOG2E * jnp.log(ratio), 3)
            extra = jnp.zeros((funds, LANES), F32)
            for k in range(6):
                extra = jnp.where(which == k, d[k], extra)
            full = jnp.concatenate([w1, w2, w1, w2, w1, w3, extra, jnp.zeros_like(extra)], axis=0)
            loads[:, c * LANES:(c + 1) * LANES] = full.astype(BF16)

    def value(i, loads):
        right = loads[...]
        total = None
        for h in range(horizon):
            reach = jnp.zeros((8, group * LANES), F32)
            for s in range(trials // step):
                left = paths_ref[h * trials + s * step:h * trials + (s + 1) * step, :]
                kept = jnp.exp2(jnp.minimum(dot(left, right), 0.0))
                reach = reach + jnp.sum(kept.reshape(step // 8, 8, group * LANES), axis=0)
            part = (float(trials) - jnp.sum(reach, axis=0, keepdims=True)) * (DISCOUNT ** (h + 1) / trials)
            total = part if total is None else total + part
        for c in range(group):
            row = pl.ds(i * group + c, 1)
            cost_ref[row, :] = total[:, c * LANES:(c + 1) * LANES] * money[row, :]

    turns = owned // group
    prepare(0, loads)

    def pair(j, _):
        prepare(2 * j + 1, spare)
        value(2 * j, loads)
        prepare(jnp.minimum(2 * j + 2, turns - 1), loads)
        value(2 * j + 1, spare)
        return 0

    lax.fori_loop(0, turns // 2, pair, 0)


def lapse_kernel(n_proj, hot_ref, level_ref, *rest):
    costs, (out_hbm, out, sem) = rest[:n_proj], rest[n_proj:]
    factors = jnp.concatenate(
        [halves(LAPSE_FLOOR + LAPSE_SPAN * jax.nn.sigmoid(LAPSE_SLOPE * (LAPSE_PIVOT - cost[...]))) for cost in costs],
        axis=0)
    chunk = 2 * LANES

    def flush(i):
        span = pl.ds(i * chunk, chunk)
        return pltpu.make_async_copy(out.at[span], out_hbm.at[span], sem.at[i])

    chunks = out.shape[0] // chunk
    for i in range(chunks):
        span = slice(i * chunk, (i + 1) * chunk)
        out[span, :] = level_ref[span, :] * join(dot(hot_ref[span, :], factors))
        flush(i).start()
    for i in range(chunks):
        flush(i).wait()


def exchange(x, axis, offset):
    return lax.ppermute(x, axis, flips(lax.axis_size(axis), offset))


def flips(n, offset):
    return [(i, i ^ offset) for i in range(n)]


def body(fund_value, in_force, guarantee_base, lapse_rate, cohort, product, guarantee_type, returns, mix_table,
         fee_table, rollup_table, fund_vol, closing_sigma_figure, shocks, base_table, year_index):
    n_proj, n_scen = lax.axis_size("proj"), lax.axis_size("scen")
    points, width = fund_value.shape
    funds, months, _ = returns.shape
    horizon = shocks.shape[1]
    products, types = mix_table.shape[0], fee_table.shape[0]
    owned = COHORTS // n_proj
    rows = -(-points // n_proj // LANES) * LANES
    message = rows + owned + 8 * (rows // LANES)
    blocks = points // LANES
    me = lax.axis_index("proj").astype(I32).reshape(1)
    plane = jax.ShapeDtypeStruct((points, width), F32)
    labels = cohort.reshape(blocks, LANES)
    mix = mix_table.T

    sheets = jnp.concatenate([shocks[None], exchange(shocks[None], "scen", 1)], axis=0)
    outs = pl.pallas_call(
        functools.partial(project_kernel, (n_proj, owned, rows, months, products, types)),
        out_shape=[pltpu.VMEM((message, width), F32)] * n_proj + [pltpu.VMEM((points, width), F32)] + [plane] * 3,
        in_specs=[SMEM] * 4 + [VMEM] * 6 + [HBM] * 4,
        out_specs=[VMEM] * (n_proj + 1) + [HBM] * 3,
        scratch_shapes=[pltpu.VMEM((points, width), F32)] * 5 + [
            pltpu.VMEM((3 * products * types, (months + 2) * LANES), BF16),
            pltpu.VMEM((points, 3 * products * types), BF16),
            pltpu.VMEM((points, 2 * width), BF16),
            pltpu.VMEM((points, 2 * width), BF16),
            pltpu.VMEM((n_proj * rows, points), BF16),
            pltpu.VMEM((COHORTS, points), BF16),
            pltpu.SemaphoreType.DMA((4,)),
            pltpu.SemaphoreType.DMA((3,)),
        ],
        compiler_params=limit(24), name="project",
    )(me, year_index, hbm(fee_table), hbm(rollup_table), hbm(labels), hbm(product.reshape(blocks, LANES)),
      hbm(guarantee_type.reshape(blocks, LANES)), hbm(mix), hbm(base_table), hbm(returns.transpose(1, 0, 2)),
      hbm(fund_value), hbm(in_force), hbm(guarantee_base), hbm(lapse_rate))
    sends, (level, fund_next, force_next, base_next) = outs[:n_proj], outs[n_proj:]

    sheets, *sends = lax.optimization_barrier((sheets, *sends))
    received = [sends[0]] + [vmem(exchange(sends[o], "proj", o)) for o in range(1, n_proj)]

    offset = 2
    while offset < n_scen:
        if 2 * offset >= n_scen:
            sheets, labels = lax.optimization_barrier((sheets, labels))
        sheets = jnp.concatenate([sheets, exchange(sheets, "scen", offset)], axis=0)
        offset *= 2
    trials = n_scen * shocks.shape[2]

    hot = pl.pallas_call(
        functools.partial(hot_kernel, owned),
        out_shape=pltpu.VMEM((points, COHORTS), BF16),
        in_specs=[SMEM, VMEM], out_specs=VMEM, compiler_params=limit(8), name="cohort_hot",
    )(me, labels)
    left = pl.pallas_call(
        paths_kernel,
        out_shape=pltpu.VMEM((horizon * trials, DEPTH), BF16),
        in_specs=[VMEM], out_specs=VMEM, compiler_params=limit(8), name="paths",
    )(vmem(sheets))
    left, hot = lax.optimization_barrier((left, hot))

    group = 16
    cost = pl.pallas_call(
        functools.partial(value_kernel, (n_proj, owned, rows, horizon, group, 64)),
        out_shape=pltpu.VMEM((owned, width), F32),
        in_specs=[SMEM] + [VMEM] * (3 + n_proj), out_specs=VMEM,
        scratch_shapes=[
            pltpu.VMEM((n_proj * rows, 2 * width), BF16),
            pltpu.VMEM((2, n_proj * rows // LANES, funds, LANES), F32),
            pltpu.VMEM((DEPTH, group * LANES), BF16),
            pltpu.VMEM((DEPTH, group * LANES), BF16),
            pltpu.VMEM((owned, width), F32),
        ],
        compiler_params=limit(24), name="value",
    )(hbm(fund_vol), hbm(closing_sigma_figure.reshape(1, width)), hbm(mix), left, *received)

    costs = [cost] + [vmem(lax.ppermute(cost, "proj", flips(n_proj, o))) for o in range(1, n_proj)]
    lapse_next = pl.pallas_call(
        functools.partial(lapse_kernel, n_proj),
        out_shape=plane, in_specs=[VMEM] * (2 + n_proj), out_specs=HBM,
        scratch_shapes=[pltpu.VMEM((points, width), F32), pltpu.SemaphoreType.DMA((points // (2 * LANES),))],
        compiler_params=limit(16), name="lapse",
    )(hot, level, *costs)
    return fund_next, force_next, base_next, lapse_next, cost


def solution(mesh):
    both, proj = P("proj", "scen"), P("proj")
    paths = P(None, None, "scen")
    placed = (both,) * 4 + (proj,) * 3 + (paths, P(), P(), P(), P(), P("scen"), paths, P(), P())
    return jax.shard_map(body, mesh=mesh, in_specs=placed, out_specs=(both,) * 5, check_vma=False)
```

profile of v0, /device:TPU:0, one launch (start us, length us, event | category | flops | bytes accessed | tf_op | source)
XLA Modules:
  0.0 52.8 jit_solution(17989462163012579068)
XLA Ops:
  0.6 3.1 %collective-permute-start = (f32[1,8,2,128]{3,2,1,0:T(2,128)}, f32[1,8,2,128]{3,2,1,0:T(2,128)S(1)}, u32[]{:S(2)}, u32[]{:S(2)}) collective-permute-start(f32[1,8,2,128]{3,2,1,0:T(2,128)} %bitcast.13), channel_id=1, source_target_pairs={{0,1},{1,0},{2,3},{3,2},{4,5},{5,4},{6,7},{7,6},{8,9},{9,8},{10,11... | collective-permute-start | bytes 24584 | tf_op jit(solution)/shard_map/ppermute | solution.py:332
  4.3 0.0 copy-start.1
  4.4 5.8 %project.1 = (f32[400,128]{1,0:T(8,128)S(1)}, f32[400,128]{1,0:T(8,128)S(1)}, f32[400,128]{1,0:T(8,128)S(1)}, f32[400,128]{1,0:T(8,128)S(1)}, f32[1024,128]{1,0:...) custom-call(s32[1]{0:T(128)} %bitcast.me_ref, s32[1]{0:T(128)S(6)} %copy.22.year_ref, ...), custom_call_target="tpu_custom_call" | custom-call | tf_op jit(solution)/shard_map/project/pallas_call | solution.py:356
  10.1 0.0 collective-permute-done
  10.1 0.0 copy-done.1
  10.2 0.0 copy-start
  10.2 1.6 %collective-permute-start.1 = (f32[2,8,2,128]{3,2,1,0:T(2,128)S(1)}, f32[2,8,2,128]{3,2,1,0:T(2,128)S(1)}, u32[]{:S(2)}, u32[]{:S(2)}) collective-permute-start(f32[2,8,2,128]{3,2,1,0:T(2,128)S(1)} %pad_maximum_fusion.2), channel_id=1, source_target_pairs={{0,2},{1,3},{2,0},{3,1},{4,6},{5,7},{6,4},{7,5},{8,10},{9,11},{10,... | collective-permute-start | bytes 49160 | tf_op jit(solution)/shard_map/ppermute | solution.py:332
  11.8 0.0 collective-permute-start.3
  11.8 1.5 %collective-permute-start.4 = (f32[400,128]{1,0:T(8,128)S(1)}, f32[400,128]{1,0:T(8,128)S(1)}, u32[]{:S(2)}, u32[]{:S(2)}) collective-permute-start(f32[400,128]{1,0:T(8,128)S(1)} %get-tuple-element.37), channel_id=1, source_target_pairs={{0,16},{8,24},{16,0},{24,8},{1,17},{9,25},{17,1},{25,9},{2,18},{10... | collective-permute-start | bytes 614408 | tf_op jit(solution)/shard_map/ppermute | solution.py:332
  13.3 0.4 collective-permute-start.5
  13.7 0.3 collective-permute-done.1
  14.0 2.6 %collective-permute-start.2 = (f32[4,8,2,128]{3,2,1,0:T(2,128)S(1)}, f32[4,8,2,128]{3,2,1,0:T(2,128)S(1)}, u32[]{:S(2)}, u32[]{:S(2)}) collective-permute-start(f32[4,8,2,128]{3,2,1,0:T(2,128)S(1)} %pad_maximum_fusion.1), channel_id=1, source_target_pairs={{0,4},{1,5},{2,6},{3,7},{4,0},{5,1},{6,2},{7,3},{8,12},{9,13},{10,... | collective-permute-start | bytes 98312 | tf_op jit(solution)/shard_map/ppermute | solution.py:332
  16.7 0.0 copy-done
  16.7 0.3 cohort_hot.1.hot_ref
  17.0 1.9 %collective-permute-done.2 = f32[4,8,2,128]{3,2,1,0:T(2,128)S(1)} collective-permute-done((f32[4,8,2,128]{3,2,1,0:T(2,128)S(1)}, f32[4,8,2,128]{3,2,1,0:T(2,128)S(1)}, u32[]{:S(2)}, u32[]{:S(2)}) %collective-permute-start.2) | collective-permute-done | bytes 32800 | tf_op jit(solution)/shard_map/ppermute | solution.py:332
  18.9 0.4 paths.1.paths_ref
  19.3 0.0 collective-permute-done.3.rest_1_
  19.3 0.5 collective-permute-done.4.rest_2_
  19.8 3.5 %collective-permute-done.5.rest_3_ = f32[400,128]{1,0:T(8,128)S(1)} collective-permute-done((f32[400,128]{1,0:T(8,128)S(1)}, f32[400,128]{1,0:T(8,128)S(1)}, u32[]{:S(2)}, u32[]{:S(2)}) %collective-permute-start.5) | collective-permute-done | bytes 204832 | tf_op jit(solution)/shard_map/ppermute | solution.py:332
  23.2 22.5 %value.1.rest_0_ = f32[128,128]{1,0:T(8,128)S(1)} custom-call(f32[8]{0:T(128)} %vol_ref.1, f32[1,128]{1,0:T(1,128)} %bitcast.17, f32[8,16]{1,0:T(8,128)} %bitcast.12, bf16[2048,64]{1,0:T(8,128)(2,1)S(1)} %paths.1.paths_ref, f32[400,128]{1,0:T(8,128)S(1)} %get-tuple-element.35.rest_0_, f32[400,128]{1,0:T(8,128)S(1)} %collective-permute-done.3.rest_1_, ...), custom_call_target="tpu_custom_call" | custom-call | tf_op jit(solution)/shard_map/value/pallas_call | solution.py:401
  45.7 1.4 %collective-permute-start.8 = (f32[128,128]{1,0:T(8,128)S(1)}, f32[128,128]{1,0:T(8,128)S(1)}, u32[]{:S(2)}, u32[]{:S(2)}) collective-permute-start(f32[128,128]{1,0:T(8,128)S(1)} %value.1.rest_0_), channel_id=1, source_target_pairs={{0,24},{8,16},{16,8},{24,0},{1,25},{9,17},{17,9},{25,1},{2,26},{10... | collective-permute-start | bytes 196616 | tf_op jit(solution)/shard_map/ppermute | solution.py:415
  47.2 0.5 %collective-permute-start.7 = (f32[128,128]{1,0:T(8,128)S(1)}, f32[128,128]{1,0:T(8,128)S(1)}, u32[]{:S(2)}, u32[]{:S(2)}) collective-permute-start(f32[128,128]{1,0:T(8,128)S(1)} %value.1.rest_0_), channel_id=1, source_target_pairs={{0,16},{8,24},{16,0},{24,8},{1,17},{9,25},{17,1},{25,9},{2,18},{10... | collective-permute-start | bytes 196616 | tf_op jit(solution)/shard_map/ppermute | solution.py:415
  47.7 0.0 collective-permute-start.6
  47.7 0.6 %copy.21 = f32[128,128]{1,0:T(8,128)} copy(f32[128,128]{1,0:T(8,128)S(1)} %value.1.rest_0_) | data formatting | bytes 131072
  48.3 1.4 %collective-permute-done.8.rest_3_ = f32[128,128]{1,0:T(8,128)S(1)} collective-permute-done((f32[128,128]{1,0:T(8,128)S(1)}, f32[128,128]{1,0:T(8,128)S(1)}, u32[]{:S(2)}, u32[]{:S(2)}) %collective-permute-start.8) | collective-permute-done | bytes 65568 | tf_op jit(solution)/shard_map/ppermute | solution.py:415
  49.7 1.9 %collective-permute-done.7.rest_2_ = f32[128,128]{1,0:T(8,128)S(1)} collective-permute-done((f32[128,128]{1,0:T(8,128)S(1)}, f32[128,128]{1,0:T(8,128)S(1)}, u32[]{:S(2)}, u32[]{:S(2)}) %collective-permute-start.7) | collective-permute-done | bytes 65568 | tf_op jit(solution)/shard_map/ppermute | solution.py:415
  51.6 0.0 collective-permute-done.6.rest_1_
  51.6 1.2 %lapse.1 = f32[1024,128]{1,0:T(8,128)} custom-call(bf16[1024,512]{1,0:T(8,128)(2,1)S(1)} %cohort_hot.1.hot_ref, f32[1024,128]{1,0:T(8,128)S(1)} %get-tuple-element.33.level_ref, f32[128,128]{1,0:T(8,128)S(1)} %value.1.rest_0_, f32[128,128]{1,0:T(8,128)S(1)} %collective-permute-done.6.rest_1_, f32[128,128]{1,0:T(8,128)S(1)} %collective-permute-done.7.rest_2_, ...), custom_call_target="tpu_custom_call" | custom-call | tf_op jit(solution)/shard_map/lapse/pallas_call | solution.py:416
  (3 shorter events, 0.1 us)
Async XLA Ops:
  0.6 9.5 %collective-permute-start = (f32[1,8,2,128]{3,2,1,0:T(2,128)}, f32[1,8,2,128]{3,2,1,0:T(2,128)S(1)}, u32[]{:S(2)}, u32[]{:S(2)}) collective-permute-start(f32[1,8,2,128]{3,2,1,0:T(2,128)} %bitcast.13), channel_id=1, source_target_pairs={{0,1},{1,0},{2,3},{3,2},{4,5},{5,4},{6,7},{7,6},{8,9},{9,8},{10,11... | collective-permute-start | bytes 24584 | tf_op jit(solution)/shard_map/ppermute | solution.py:332
  4.3 5.8 %copy-start.1 = (f32[8,2,128]{2,1,0:T(2,128)S(1)}, f32[8,2,128]{2,1,0:T(2,128)}, u32[]{:S(2)}) copy-start(f32[8,2,128]{2,1,0:T(2,128)} %param.29) | copy-start | bytes 24580
  10.2 6.5 %copy-start = (s32[1024]{0:T(1024)S(1)}, s32[1024]{0:T(1024)}, u32[]{:S(2)}) copy-start(s32[1024]{0:T(1024)} %param.20) | copy-start | bytes 12292
  10.2 3.8 %collective-permute-start.1 = (f32[2,8,2,128]{3,2,1,0:T(2,128)S(1)}, f32[2,8,2,128]{3,2,1,0:T(2,128)S(1)}, u32[]{:S(2)}, u32[]{:S(2)}) collective-permute-start(f32[2,8,2,128]{3,2,1,0:T(2,128)S(1)} %pad_maximum_fusion.2), channel_id=1, source_target_pairs={{0,2},{1,3},{2,0},{3,1},{4,6},{5,7},{6,4},{7,5},{8,10},{9,11},{10,... | collective-permute-start | bytes 49160 | tf_op jit(solution)/shard_map/ppermute | solution.py:332
  11.8 7.5 %collective-permute-start.3 = (f32[400,128]{1,0:T(8,128)S(1)}, f32[400,128]{1,0:T(8,128)S(1)}, u32[]{:S(2)}, u32[]{:S(2)}) collective-permute-start(f32[400,128]{1,0:T(8,128)S(1)} %get-tuple-element.36), channel_id=1, source_target_pairs={{0,8},{8,0},{16,24},{24,16},{1,9},{9,1},{17,25},{25,17},{2,10},{10... | collective-permute-start | bytes 614408 | tf_op jit(solution)/shard_map/ppermute | solution.py:332
  11.8 8.0 %collective-permute-start.4 = (f32[400,128]{1,0:T(8,128)S(1)}, f32[400,128]{1,0:T(8,128)S(1)}, u32[]{:S(2)}, u32[]{:S(2)}) collective-permute-start(f32[400,128]{1,0:T(8,128)S(1)} %get-tuple-element.37), channel_id=1, source_target_pairs={{0,16},{8,24},{16,0},{24,8},{1,17},{9,25},{17,1},{25,9},{2,18},{10... | collective-permute-start | bytes 614408 | tf_op jit(solution)/shard_map/ppermute | solution.py:332
  13.3 9.9 %collective-permute-start.5 = (f32[400,128]{1,0:T(8,128)S(1)}, f32[400,128]{1,0:T(8,128)S(1)}, u32[]{:S(2)}, u32[]{:S(2)}) collective-permute-start(f32[400,128]{1,0:T(8,128)S(1)} %get-tuple-element.38), channel_id=1, source_target_pairs={{0,24},{8,16},{16,8},{24,0},{1,25},{9,17},{17,9},{25,1},{2,26},{10... | collective-permute-start | bytes 614408 | tf_op jit(solution)/shard_map/ppermute | solution.py:332
  14.0 4.9 %collective-permute-start.2 = (f32[4,8,2,128]{3,2,1,0:T(2,128)S(1)}, f32[4,8,2,128]{3,2,1,0:T(2,128)S(1)}, u32[]{:S(2)}, u32[]{:S(2)}) collective-permute-start(f32[4,8,2,128]{3,2,1,0:T(2,128)S(1)} %pad_maximum_fusion.1), channel_id=1, source_target_pairs={{0,4},{1,5},{2,6},{3,7},{4,0},{5,1},{6,2},{7,3},{8,12},{9,13},{10,... | collective-permute-start | bytes 98312 | tf_op jit(solution)/shard_map/ppermute | solution.py:332
  45.7 4.0 %collective-permute-start.8 = (f32[128,128]{1,0:T(8,128)S(1)}, f32[128,128]{1,0:T(8,128)S(1)}, u32[]{:S(2)}, u32[]{:S(2)}) collective-permute-start(f32[128,128]{1,0:T(8,128)S(1)} %value.1.rest_0_), channel_id=1, source_target_pairs={{0,24},{8,16},{16,8},{24,0},{1,25},{9,17},{17,9},{25,1},{2,26},{10... | collective-permute-start | bytes 196616 | tf_op jit(solution)/shard_map/ppermute | solution.py:415
  47.2 4.4 %collective-permute-start.7 = (f32[128,128]{1,0:T(8,128)S(1)}, f32[128,128]{1,0:T(8,128)S(1)}, u32[]{:S(2)}, u32[]{:S(2)}) collective-permute-start(f32[128,128]{1,0:T(8,128)S(1)} %value.1.rest_0_), channel_id=1, source_target_pairs={{0,16},{8,24},{16,0},{24,8},{1,17},{9,25},{17,1},{25,9},{2,18},{10... | collective-permute-start | bytes 196616 | tf_op jit(solution)/shard_map/ppermute | solution.py:415
  47.7 3.9 %collective-permute-start.6 = (f32[128,128]{1,0:T(8,128)S(1)}, f32[128,128]{1,0:T(8,128)S(1)}, u32[]{:S(2)}, u32[]{:S(2)}) collective-permute-start(f32[128,128]{1,0:T(8,128)S(1)} %value.1.rest_0_), channel_id=1, source_target_pairs={{0,8},{8,0},{16,24},{24,16},{1,9},{9,1},{17,25},{25,17},{2,10},{10... | collective-permute-start | bytes 196616 | tf_op jit(solution)/shard_map/ppermute | solution.py:415
where the time goes:
time: 53 us; the launch traced here: 52.8 us
  Pallas kernels  30.1 us (57%)
  starting transfers between devices  11.2 us (21%)
  waiting for transfers between devices  9.4 us (18%)
  between operations  1.37 us (3%)
  local copies, waits for them, and re-layouts  0.64 us (1%)
    pallas_call x1, Pallas kernels, body(): pl.pallas_call(functools.partial(value_kernel, (n_proj, owned, rows, hori...  22.5 us
    ppermute x6, starting transfers between devices, exchange(): return lax.ppermute(x, axis, flips(lax.axis_size(axis), offset))  9.21 us
    ppermute x6, waiting for transfers between devices, exchange(): return lax.ppermute(x, axis, flips(lax.axis_size(axis), offset))  6.15 us
    pallas_call x1, Pallas kernels, body(): pl.pallas_call(functools.partial(project_kernel, (n_proj, owned, rows, mo...  5.77 us
    ppermute x3, waiting for transfers between devices, body(): lax.ppermute(cost, 'proj', flips(n_proj, o))  3.25 us
    ppermute x3, starting transfers between devices, body(): lax.ppermute(cost, 'proj', flips(n_proj, o))  1.98 us
    pallas_call x1, Pallas kernels, body(): pl.pallas_call(functools.partial(lapse_kernel, n_proj), out_shape=plane,...  1.19 us
  transfers between devices with their start and end apart: 9, of which 6 were waited for; matrix products, arithmetic and copies ran while one was open for 1% of the time, Pallas kernels for 12%

commit v1 on v0

--- a/solution.py
+++ b/solution.py
@@ -19,7 +19,6 @@
 HIGHEST = lax.Precision.HIGHEST
 F32, BF16, I32 = jnp.float32, jnp.bfloat16, jnp.int32
 VMEM = pl.BlockSpec(memory_space=pltpu.VMEM)
-SMEM = pl.BlockSpec(memory_space=pltpu.SMEM)
 HBM = pl.BlockSpec(memory_space=pltpu.HBM)
 
 
@@ -48,8 +47,8 @@
     return x[:, :LANES] + x[:, LANES:]
 
 
-def onehot(row, shape):
-    return (iota(shape, 0) == row).astype(BF16)
+def onehot(row, ramp):
+    return jnp.where(ramp == row, 1.0, 0.0).astype(BF16)
 
 
 def vmem(x):
@@ -70,58 +69,31 @@
     return owner, lax.shift_left(owner, shift) + jnp.bitwise_and(cohort, owned - 1)
 
 
-def project_kernel(dims, me_ref, year_ref, fee_ref, roll_ref, cohort_ref, product_ref, type_ref, mix_ref, base_ref,
-                   returns_ref, fund_hbm, force_hbm, guar_hbm, lapse_hbm, *rest):
-    n_proj, owned, rows, months, products, types = dims
-    sends = rest[:n_proj]
-    (level_ref, fund_out, force_out, guar_out, fund, force, guar, lapse, grow, table, hot, weighted, secured,
-     move, gather, in_sem, out_sem) = rest[n_proj:]
+def project_kernel(dims, *refs):
+    n_proj, owned, rows = dims
+    small, big = refs[:7], refs[7:11]
+    sends, refs = refs[11:11 + n_proj], refs[11 + n_proj:]
+    results, local_small, planes = refs[:3], refs[3:10], refs[10:14]
+    table, hot, weighted, secured, move, gather, ramp, small_sem, in_sem = refs[14:]
+    cohort_ref, product_ref, type_ref, fee_ref, roll_ref, mix_ref, returns_ref = local_small
+    fund, force, guar, lapse = planes
     points = fund.shape[0]
     blocks = points // LANES
+    months = returns_ref.shape[0]
+    products, types = mix_ref.shape[1], fee_ref.shape[1]
     combos = products * types
-    sources = ((fund_hbm, fund), (guar_hbm, guar), (lapse_hbm, lapse), (force_hbm, force))
-    sinks = ((fund, fund_out), (guar, guar_out), (force, force_out))
-
-    def fetch(a):
-        return pltpu.make_async_copy(*sources[a], in_sem.at[a])
-
-    def flush(a):
-        return pltpu.make_async_copy(*sinks[a], out_sem.at[a])
-
-    for a in range(4):
-        fetch(a).start()
-
-    combo_product = lax.shift_right_logical(iota((combos, products), 0), types.bit_length() - 1)
-    pick = (combo_product == iota((combos, products), 1)).astype(F32)
-    mix = mix_ref[...].T
-    mix = mix / jnp.sum(mix, axis=1, keepdims=True)
-    mix = jnp.dot(pick, mix, precision=HIGHEST, preferred_element_type=F32)
-    combo_type = jnp.bitwise_and(iota((combos, LANES), 0), types - 1)
-    fee = jnp.zeros((combos, LANES), F32)
-    roll = jnp.zeros((combos, LANES), F32)
-    for g in range(types):
-        fee = jnp.where(combo_type == g, fee_ref[g], fee)
-        roll = jnp.where(combo_type == g, roll_ref[g], roll)
-    keep = 1.0 - fee
-
-    def put(column, value):
-        for i, part in enumerate(split(value, 3)):
-            table[i * combos:(i + 1) * combos, column * LANES:(column + 1) * LANES] = part.astype(BF16)
-
-    for t in range(months):
-        growth = 1.0 + jnp.dot(mix, returns_ref[t], precision=HIGHEST, preferred_element_type=F32)
-        put(t, growth * keep)
-    put(months, 1.0 + roll / MONTHS_PER_YEAR)
-    level = jnp.sum(pick * base_ref[pl.ds(year_ref[0], 1), :], axis=1, keepdims=True)
-    put(months + 1, jnp.broadcast_to(level, (combos, LANES)))
-
-    combo = (product_ref[...] * types + type_ref[...]).astype(F32).T
-    slot = jnp.bitwise_and(iota((LANES, 3 * combos), 1), combos - 1).astype(F32)
-    for b in range(blocks):
-        column = jnp.broadcast_to(combo[:, b:b + 1], (LANES, 3 * combos))
-        hot[b * LANES:(b + 1) * LANES, :] = (column == slot).astype(BF16)
-
-    owner = relabel(cohort_ref[...], owned, me_ref[0])[0]
+
+    reads = [pltpu.make_async_copy(small[i], local_small[i], small_sem.at[i]) for i in range(7)]
+    loads = [pltpu.make_async_copy(big[i], planes[i], in_sem.at[i]) for i in range(4)]
+    for copy in reads + loads:
+        copy.start()
+    ramp[...] = iota(ramp.shape, 0).astype(F32)
+    for copy in reads:
+        copy.wait()
+
+    cohort = cohort_ref[...]
+    owner = relabel(cohort, owned, lax.axis_index("proj"))[0]
+    local = jnp.bitwise_and(cohort, owned - 1).astype(F32)
     masks = jnp.concatenate([(owner == q).astype(F32) for q in range(n_proj)], axis=0)
     lower = (iota((LANES, LANES), 0) < iota((LANES, LANES), 1)).astype(BF16)
     before = dot(masks.astype(BF16), lower)
@@ -131,74 +103,93 @@
     shift = blocks.bit_length() - 1
     ahead = (lax.shift_right_logical(r, shift) == lax.shift_right_logical(c, shift)) & (c < r)
     before = before + dot(ahead.astype(BF16), count.astype(BF16))
-    place = jnp.zeros((blocks, LANES), F32)
-    for q in range(n_proj):
-        span = slice(q * blocks, (q + 1) * blocks)
-        place = place + masks[span] * before[span]
-
-    local = jnp.bitwise_and(cohort_ref[...], owned - 1)
-    place = place.astype(I32)
+
+    mix = mix_ref[...].T
+    mix = mix / jnp.sum(mix, axis=1, keepdims=True)
+    shares = [jnp.broadcast_to(mix[:, f:f + 1], (products, LANES)) for f in range(mix.shape[1])]
+    wide = (products, LANES)
+    keeps = [jnp.broadcast_to(1.0 - fee_ref[:, g:g + 1], wide) for g in range(types)]
+    rolls = [jnp.broadcast_to(1.0 + roll_ref[:, g:g + 1] / MONTHS_PER_YEAR, wide) for g in range(types)]
+    held = [jnp.ones(wide, F32)] * types
+    best = [jnp.zeros(wide, F32)] * types
+    rolled = [jnp.ones(wide, F32)] * types
+    for t in range(months):
+        month = returns_ref[t]
+        growth = 1.0 + sum(share * month[f:f + 1] for f, share in enumerate(shares))
+        for g in range(types):
+            held[g] = held[g] * growth * keeps[g]
+            best[g] = jnp.maximum(best[g] * rolls[g], held[g])
+            rolled[g] = rolled[g] * rolls[g]
+    for column, value in enumerate((held, best, rolled)):
+        for i, part in enumerate(split(jnp.concatenate(value, axis=0), 3)):
+            table[i * combos:(i + 1) * combos, column * LANES:(column + 1) * LANES] = part.astype(BF16)
+
+    combo = (type_ref[...] * products + product_ref[...]).astype(F32).T
+    slot = iota((LANES, 3 * combos), 1)
+    slot = (slot - combos * ((slot >= combos).astype(I32) + (slot >= 2 * combos).astype(I32))).astype(F32)
+    for b in range(blocks):
+        column = jnp.broadcast_to(combo[:, b:b + 1], slot.shape)
+        hot[b * LANES:(b + 1) * LANES, :] = onehot(column, slot)
+
+    for o in range(n_proj):
+        mine = masks[o * blocks:(o + 1) * blocks] > 0.0
+        rank = jnp.where(mine, before[o * blocks:(o + 1) * blocks], -1.0)
+        label = jnp.where(mine, local, -1.0)
+        for b in range(blocks):
+            span = slice(b * LANES, (b + 1) * LANES)
+            move[o * rows:(o + 1) * rows, span] = onehot(rank[b:b + 1], ramp[:rows, :])
+            gather[o * owned:(o + 1) * owned, span] = onehot(label[b:b + 1], ramp[:owned, :])
     kind = product_ref[...].astype(F32)
     which = iota((16, LANES), 0)
     facts = jnp.concatenate(
-        [jnp.where(which == 0, kind[b:b + 1], jnp.where(which == 1, local[b:b + 1].astype(F32), 0.0)) for b in range(blocks)],
+        [jnp.where(which == 0, kind[b:b + 1], jnp.where(which == 1, local[b:b + 1], 0.0)) for b in range(blocks)],
         axis=1).astype(BF16)
-    for o in range(n_proj):
-        mine = owner == o
-        rank = jnp.where(mine, place, -1)
-        label = jnp.where(mine, local, -1)
-        for b in range(blocks):
-            span = slice(b * LANES, (b + 1) * LANES)
-            move[o * rows:(o + 1) * rows, span] = onehot(rank[b:b + 1], (rows, LANES))
-            gather[o * owned:(o + 1) * owned, span] = onehot(label[b:b + 1], (owned, LANES))
-    tail = dot(hot[...], table[:, months * LANES:])
-    grow[...] = tail[:, :LANES]
-    level_ref[...] = tail[:, LANES:]
-    for a in range(2):
-        fetch(a).wait()
-    for t in range(0, months, 2):
-        factors = dot(hot[...], table[:, t * LANES:(t + 2) * LANES])
-        f = fund[...] * factors[:, :LANES]
-        g = jnp.maximum(guar[...] * grow[...], f)
-        f = f * factors[:, LANES:]
-        guar[...] = jnp.maximum(g * grow[...], f)
-        fund[...] = f
-    flush(0).start()
-    flush(1).start()
-    for a in range(2, 4):
-        fetch(a).wait()
+    told = lax.dot_general(facts, move[...], (((1,), (1,)), ((), ())), preferred_element_type=F32)
+
+    for copy in loads:
+        copy.wait()
+    factors = dot(hot[...], table[...])
     stay = 1.0 - lapse[...] / MONTHS_PER_YEAR
     stay = stay * stay * stay
     stay = stay * stay
     n = force[...] * (stay * stay)
-    force[...] = n
-    flush(2).start()
-    weighted[...] = halves(n * fund[...])
-    secured[...] = halves(n * guar[...])
-
+    f = fund[...]
+    g = jnp.maximum(guar[...] * factors[:, 2 * LANES:3 * LANES], f * factors[:, LANES:2 * LANES])
+    f = f * factors[:, :LANES]
+    for result, value in zip(results, (f, n, g)):
+        result[...] = value
+    weighted[...] = halves(n * f)
+    secured[...] = halves(n * g)
     moved = join(dot(move[...], weighted[...]))
     summed = join(dot(gather[...], secured[...]))
-    told = lax.dot_general(facts, move[...], (((1,), (1,)), ((), ())), preferred_element_type=F32)
     for o in range(n_proj):
         send = sends[o]
         send[:rows, :] = moved[o * rows:(o + 1) * rows]
         send[rows:rows + owned, :] = summed[o * owned:(o + 1) * owned]
         for b in range(rows // LANES):
-            start = rows + owned + 8 * b
+            start = rows + owned + 2 * b
             first = o * rows + b * LANES
-            send[start:start + 8, :] = told[:8, first:first + LANES]
-
-    for a in range(3):
-        flush(a).wait()
-
-
-def hot_kernel(owned, me_ref, cohort_ref, hot_ref):
-    _, label = relabel(cohort_ref[...], owned, me_ref[0])
+            send[start:start + 2, :] = told[:2, first:first + LANES]
+
+
+def hot_kernel(owned, year_ref, cohort_ref, product_ref, base_ref, *refs):
+    planes, (hot_ref, level_ref), results, sem = refs[:3], refs[3:5], refs[5:8], refs[8]
+    stores = [pltpu.make_async_copy(planes[i], results[i], sem.at[i]) for i in range(3)]
+    for copy in stores:
+        copy.start()
+    _, label = relabel(cohort_ref[...], owned, lax.axis_index("proj"))
     label = label.astype(F32).T
+    product = product_ref[...].astype(F32).T
     slot = iota((LANES, hot_ref.shape[1]), 1).astype(F32)
+    rates = base_ref[pl.ds(year_ref[0], 1), :]
     for b in range(hot_ref.shape[0] // LANES):
-        column = jnp.broadcast_to(label[:, b:b + 1], slot.shape)
-        hot_ref[b * LANES:(b + 1) * LANES, :] = (column == slot).astype(BF16)
+        span = slice(b * LANES, (b + 1) * LANES)
+        hot_ref[span, :] = onehot(jnp.broadcast_to(label[:, b:b + 1], slot.shape), slot)
+        kind = jnp.broadcast_to(product[:, b:b + 1], (LANES, rates.shape[1]))
+        rate = jnp.sum(jnp.where(kind == slot[:, :rates.shape[1]], rates, 0.0), axis=1, keepdims=True)
+        level_ref[span, :] = jnp.broadcast_to(rate, (LANES, LANES))
+    for copy in stores:
+        copy.wait()
 
 
 def paths_kernel(shocks_ref, paths_ref):
@@ -230,8 +221,8 @@
     for o in range(n_proj):
         weighted[o * rows:(o + 1) * rows, :] = halves(received[o][:rows, :])
         for b in range(per):
-            start = rows + owned + 8 * b
-            facts = received[o][start:start + 8, :]
+            start = rows + owned + 2 * b
+            facts = received[o][start:start + 2, :]
             hot = (jnp.broadcast_to(facts[0:1], (products, LANES)).astype(I32) == iota((products, LANES), 0)).astype(F32)
             share = lax.dot_general(mix, hot, (((1,), (0,)), ((), ())), precision=HIGHEST, preferred_element_type=F32)
             top, low = split(share, 2)
@@ -242,9 +233,8 @@
     for b in range(spans):
         mixes[0, b] = tops[b]
         mixes[1, b] = lows[b]
-    vol = jnp.zeros((funds, LANES), F32)
-    for f in range(funds):
-        vol = jnp.where(iota((funds, LANES), 0) == f, vol_ref[f], vol)
+    same = (iota((funds, funds), 0) == iota((funds, funds), 1)).astype(F32)
+    vol = jnp.broadcast_to(jnp.sum(same * vol_ref[...], axis=1, keepdims=True), (funds, LANES))
     sigma = sigma_ref[...]
     scale = sigma * LOG2E
     slope = -0.5 * sigma * sigma * LOG2E
@@ -340,39 +330,41 @@
          fee_table, rollup_table, fund_vol, closing_sigma_figure, shocks, base_table, year_index):
     n_proj, n_scen = lax.axis_size("proj"), lax.axis_size("scen")
     points, width = fund_value.shape
-    funds, months, _ = returns.shape
+    funds, _, _ = returns.shape
     horizon = shocks.shape[1]
     products, types = mix_table.shape[0], fee_table.shape[0]
     owned = COHORTS // n_proj
     rows = -(-points // n_proj // LANES) * LANES
-    message = rows + owned + 8 * (rows // LANES)
+    message = rows + owned + 8 * -(-2 * (rows // LANES) // 8)
     blocks = points // LANES
-    me = lax.axis_index("proj").astype(I32).reshape(1)
     plane = jax.ShapeDtypeStruct((points, width), F32)
     labels = cohort.reshape(blocks, LANES)
     mix = mix_table.T
 
     sheets = jnp.concatenate([shocks[None], exchange(shocks[None], "scen", 1)], axis=0)
+    kinds = product.reshape(blocks, LANES)
+    small = [labels, kinds, guarantee_type.reshape(blocks, LANES), fee_table.reshape(1, types),
+             rollup_table.reshape(1, types), mix, returns.transpose(1, 0, 2)]
+    big = [fund_value, in_force, guarantee_base, lapse_rate]
     outs = pl.pallas_call(
-        functools.partial(project_kernel, (n_proj, owned, rows, months, products, types)),
-        out_shape=[pltpu.VMEM((message, width), F32)] * n_proj + [pltpu.VMEM((points, width), F32)] + [plane] * 3,
-        in_specs=[SMEM] * 4 + [VMEM] * 6 + [HBM] * 4,
-        out_specs=[VMEM] * (n_proj + 1) + [HBM] * 3,
-        scratch_shapes=[pltpu.VMEM((points, width), F32)] * 5 + [
-            pltpu.VMEM((3 * products * types, (months + 2) * LANES), BF16),
+        functools.partial(project_kernel, (n_proj, owned, rows)),
+        out_shape=[pltpu.VMEM((message, width), F32)] * n_proj + [pltpu.VMEM((points, width), F32)] * 3,
+        in_specs=[HBM] * 11,
+        out_specs=[VMEM] * (n_proj + 3),
+        scratch_shapes=[pltpu.VMEM(x.shape, x.dtype) for x in small + big] + [
+            pltpu.VMEM((3 * products * types, 3 * LANES), BF16),
             pltpu.VMEM((points, 3 * products * types), BF16),
             pltpu.VMEM((points, 2 * width), BF16),
             pltpu.VMEM((points, 2 * width), BF16),
             pltpu.VMEM((n_proj * rows, points), BF16),
             pltpu.VMEM((COHORTS, points), BF16),
+            pltpu.VMEM((max(rows, owned), LANES), F32),
+            pltpu.SemaphoreType.DMA((7,)),
             pltpu.SemaphoreType.DMA((4,)),
-            pltpu.SemaphoreType.DMA((3,)),
         ],
         compiler_params=limit(24), name="project",
-    )(me, year_index, hbm(fee_table), hbm(rollup_table), hbm(labels), hbm(product.reshape(blocks, LANES)),
-      hbm(guarantee_type.reshape(blocks, LANES)), hbm(mix), hbm(base_table), hbm(returns.transpose(1, 0, 2)),
-      hbm(fund_value), hbm(in_force), hbm(guarantee_base), hbm(lapse_rate))
-    sends, (level, fund_next, force_next, base_next) = outs[:n_proj], outs[n_proj:]
+    )(*[hbm(x) for x in small + big])
+    sends, planes = outs[:n_proj], outs[n_proj:]
 
     sheets, *sends = lax.optimization_barrier((sheets, *sends))
     received = [sends[0]] + [vmem(exchange(sends[o], "proj", o)) for o in range(1, n_proj)]
@@ -380,16 +372,18 @@
     offset = 2
     while offset < n_scen:
         if 2 * offset >= n_scen:
-            sheets, labels = lax.optimization_barrier((sheets, labels))
+            sheets, labels, year_index = lax.optimization_barrier((sheets, labels, year_index))
         sheets = jnp.concatenate([sheets, exchange(sheets, "scen", offset)], axis=0)
         offset *= 2
     trials = n_scen * shocks.shape[2]
 
-    hot = pl.pallas_call(
+    hot, level, fund_next, force_next, base_next = pl.pallas_call(
         functools.partial(hot_kernel, owned),
-        out_shape=pltpu.VMEM((points, COHORTS), BF16),
-        in_specs=[SMEM, VMEM], out_specs=VMEM, compiler_params=limit(8), name="cohort_hot",
-    )(me, labels)
+        out_shape=[pltpu.VMEM((points, COHORTS), BF16), pltpu.VMEM((points, width), F32)] + [plane] * 3,
+        in_specs=[pl.BlockSpec(memory_space=pltpu.SMEM)] + [VMEM] * 6, out_specs=[VMEM] * 2 + [HBM] * 3,
+        scratch_shapes=[pltpu.SemaphoreType.DMA((3,))],
+        compiler_params=limit(8), name="cohort_hot",
+    )(year_index, labels, kinds, base_table, *planes)
     left = pl.pallas_call(
         paths_kernel,
         out_shape=pltpu.VMEM((horizon * trials, DEPTH), BF16),
@@ -401,7 +395,7 @@
     cost = pl.pallas_call(
         functools.partial(value_kernel, (n_proj, owned, rows, horizon, group, 64)),
         out_shape=pltpu.VMEM((owned, width), F32),
-        in_specs=[SMEM] + [VMEM] * (3 + n_proj), out_specs=VMEM,
+        in_specs=[VMEM] * (4 + n_proj), out_specs=VMEM,
         scratch_shapes=[
             pltpu.VMEM((n_proj * rows, 2 * width), BF16),
             pltpu.VMEM((2, n_proj * rows // LANES, funds, LANES), F32),
@@ -410,9 +404,13 @@
             pltpu.VMEM((owned, width), F32),
         ],
         compiler_params=limit(24), name="value",
-    )(hbm(fund_vol), hbm(closing_sigma_figure.reshape(1, width)), hbm(mix), left, *received)
-
-    costs = [cost] + [vmem(lax.ppermute(cost, "proj", flips(n_proj, o))) for o in range(1, n_proj)]
+    )(hbm(fund_vol.reshape(1, funds)), hbm(closing_sigma_figure.reshape(1, width)), hbm(mix), left, *received)
+
+    costs = [cost]
+    for o in range(1, n_proj):
+        near = o % 2 and o > 1
+        costs.append(exchange(costs[o - 1] if near else cost, "proj", 1 if near else o))
+    costs = [cost] + [vmem(x) for x in costs[1:]]
     lapse_next = pl.pallas_call(
         functools.partial(lapse_kernel, n_proj),
         out_shape=plane, in_specs=[VMEM] * (2 + n_proj), out_specs=HBM,

time: 53 us -> 50.2 us (0.947)
  waiting for transfers between devices: 9.4 us -> 7.74 us
  Pallas kernels: 30.1 us -> 29.4 us
    ppermute x3 -> x0, waiting for transfers between devices: 3.25 us -> none  [body(): lax.ppermute(cost, 'proj', flips(n_proj, o))]
    ppermute x3 -> x0, starting transfers between devices: 1.98 us -> none  [body(): lax.ppermute(cost, 'proj', flips(n_proj, o))]
    ppermute x6 -> x9, waiting for transfers between devices: 6.15 us -> 7.74 us  [exchange(): return lax.ppermute(x, axis, flips(lax.axis_size(axis), offset))]
    ppermute x6 -> x9, starting transfers between devices: 9.21 us -> 10.8 us  [exchange(): return lax.ppermute(x, axis, flips(lax.axis_size(axis), offset))]
    pallas_call x2, Pallas kernels: 6.1 us -> 5.56 us  [the longest x1 4.3 us: body(): pl.pallas_call(functools.partial(project_kernel, (n_proj, owned, rows)),...]
where the time goes in v1:
time: 50.2 us; the launch traced here: 50 us
  Pallas kernels  29.4 us (59%)
  starting transfers between devices  10.8 us (22%)
  waiting for transfers between devices  7.74 us (15%)
  between operations  1.39 us (3%)
  local copies, waits for them, and re-layouts  0.65 us (1%)
    pallas_call x1, Pallas kernels, body(): pl.pallas_call(functools.partial(value_kernel, (n_proj, owned, rows, hori...  22.3 us
    ppermute x9, starting transfers between devices, exchange(): return lax.ppermute(x, axis, flips(lax.axis_size(axis), offset))  10.8 us
    ppermute x9, waiting for transfers between devices, exchange(): return lax.ppermute(x, axis, flips(lax.axis_size(axis), offset))  7.74 us
    pallas_call x1, Pallas kernels, body(): pl.pallas_call(functools.partial(project_kernel, (n_proj, owned, rows)),...  4.3 us
    pallas_call x1, Pallas kernels, body(): pl.pallas_call(functools.partial(hot_kernel, owned), out_shape=[pltpu.VME...  1.26 us
    pallas_call x1, Pallas kernels, body(): pl.pallas_call(functools.partial(lapse_kernel, n_proj), out_shape=plane,...  1.19 us
  transfers between devices with their start and end apart: 9, of which 6 were waited for; matrix products, arithmetic and copies ran while one was open for 1% of the time, Pallas kernels for 12%

profile of v1, /device:TPU:0, one launch (start us, length us, event | category | flops | bytes accessed | tf_op | source)
XLA Modules:
  0.0 50.0 jit_solution(843293830626081663)
XLA Ops:
  0.6 3.1 %collective-permute-start = (f32[1,8,2,128]{3,2,1,0:T(2,128)}, f32[1,8,2,128]{3,2,1,0:T(2,128)S(1)}, u32[]{:S(2)}, u32[]{:S(2)}) collective-permute-start(f32[1,8,2,128]{3,2,1,0:T(2,128)} %bitcast.17), channel_id=1, source_target_pairs={{0,1},{1,0},{2,3},{3,2},{4,5},{5,4},{6,7},{7,6},{8,9},{9,8},{10,11... | collective-permute-start | bytes 24584 | tf_op jit(solution)/shard_map/ppermute | solution.py:322
  3.7 0.0 copy-start.3
  3.7 4.3 %project.1 = (f32[392,128]{1,0:T(8,128)S(1)}, f32[392,128]{1,0:T(8,128)S(1)}, f32[392,128]{1,0:T(8,128)S(1)}, f32[392,128]{1,0:T(8,128)S(1)}, f32[1024,128]{1,0:...) custom-call(s32[8,128]{1,0:T(8,128)} %bitcast.10, s32[8,128]{1,0:T(8,128)} %bitcast.12, ...), custom_call_target="tpu_custom_call" | custom-call | tf_op jit(solution)/shard_map/project/pallas_call | solution.py:349
  8.0 0.0 collective-permute-done
  8.0 0.0 copy-done.3
  8.0 1.6 %collective-permute-start.1 = (f32[2,8,2,128]{3,2,1,0:T(2,128)S(1)}, f32[2,8,2,128]{3,2,1,0:T(2,128)S(1)}, u32[]{:S(2)}, u32[]{:S(2)}) collective-permute-start(f32[2,8,2,128]{3,2,1,0:T(2,128)S(1)} %pad_maximum_fusion.2), channel_id=1, source_target_pairs={{0,2},{1,3},{2,0},{3,1},{4,6},{5,7},{6,4},{7,5},{8,10},{9,11},{10,... | collective-permute-start | bytes 49160 | tf_op jit(solution)/shard_map/ppermute | solution.py:322
  9.7 0.0 collective-permute-start.3
  9.7 1.5 %collective-permute-start.4 = (f32[392,128]{1,0:T(8,128)S(1)}, f32[392,128]{1,0:T(8,128)S(1)}, u32[]{:S(2)}, u32[]{:S(2)}) collective-permute-start(f32[392,128]{1,0:T(8,128)S(1)} %get-tuple-element.47), channel_id=1, source_target_pairs={{0,16},{8,24},{16,0},{24,8},{1,17},{9,25},{17,1},{25,9},{2,18},{10... | collective-permute-start | bytes 602120 | tf_op jit(solution)/shard_map/ppermute | solution.py:322
  11.2 0.4 collective-permute-start.5
  11.6 0.3 collective-permute-done.1
  11.9 0.0 copy-start.1
  11.9 0.0 copy-start.2
  11.9 0.0 copy-start
  11.9 2.7 %collective-permute-start.2 = (f32[4,8,2,128]{3,2,1,0:T(2,128)S(1)}, f32[4,8,2,128]{3,2,1,0:T(2,128)S(1)}, u32[]{:S(2)}, u32[]{:S(2)}) collective-permute-start(f32[4,8,2,128]{3,2,1,0:T(2,128)S(1)} %pad_maximum_fusion.1), channel_id=1, source_target_pairs={{0,4},{1,5},{2,6},{3,7},{4,0},{5,1},{6,2},{7,3},{8,12},{9,13},{10,... | collective-permute-start | bytes 98312 | tf_op jit(solution)/shard_map/ppermute | solution.py:322
  15.2 0.0 copy-done.1
  15.2 0.0 copy-done.2
  15.2 0.0 copy-done
  15.2 1.3 %cohort_hot.1 = (bf16[1024,512]{1,0:T(8,128)(2,1)S(1)}, f32[1024,128]{1,0:T(8,128)S(1)}, f32[1024,128]{1,0:T(8,128)}, f32[1024,128]{1,0:T(8,128)}, f32[1024,128]{1,0:T(8,128)}) custom-call(s32[1]{0:T(128)S(6)} %copy.22.year_ref, s32[8,128]{1,0:T(8,128)S(1)} %bitcast.11, s32[8,128]{1,0:T(8,128)S(1)} %bitcast.13, f32[10,16]{1,0:T(8,128)S(1)} %copy-done.2, ...), custom_call_target="tpu_custom_call" | custom-call | tf_op jit(solution)/shard_map/cohort_hot/pallas_call | solution.py:380
  16.5 0.3 collective-permute-done.2
  16.8 0.4 paths.1.paths_ref
  17.2 0.0 collective-permute-done.3.rest_1_
  17.2 0.4 collective-permute-done.4.rest_2_
  17.6 3.4 %collective-permute-done.5.rest_3_ = f32[392,128]{1,0:T(8,128)S(1)} collective-permute-done((f32[392,128]{1,0:T(8,128)S(1)}, f32[392,128]{1,0:T(8,128)S(1)}, u32[]{:S(2)}, u32[]{:S(2)}) %collective-permute-start.5) | collective-permute-done | bytes 200736 | tf_op jit(solution)/shard_map/ppermute | solution.py:322
  20.9 22.3 %value.1.rest_0_ = f32[128,128]{1,0:T(8,128)S(1)} custom-call(f32[1,8]{1,0:T(1,128)} %bitcast.20, f32[1,128]{1,0:T(1,128)} %bitcast.21, f32[8,16]{1,0:T(8,128)} %bitcast.16, bf16[2048,64]{1,0:T(8,128)(2,1)S(1)} %paths.1.paths_ref, f32[392,128]{1,0:T(8,128)S(1)} %get-tuple-element.45.rest_0_, f32[392,128]{1,0:T(8,128)S(1)} %collective-permute-done.3.rest_1_, ...), custom_call_target="tpu_custom_call" | custom-call | tf_op jit(solution)/shard_map/value/pallas_call | solution.py:395
  43.3 1.6 %collective-permute-start.7 = (f32[128,128]{1,0:T(8,128)S(1)}, f32[128,128]{1,0:T(8,128)S(1)}, u32[]{:S(2)}, u32[]{:S(2)}) collective-permute-start(f32[128,128]{1,0:T(8,128)S(1)} %value.1.rest_0_), channel_id=1, source_target_pairs={{0,16},{8,24},{16,0},{24,8},{1,17},{9,25},{17,1},{25,9},{2,18},{10... | collective-permute-start | bytes 196616 | tf_op jit(solution)/shard_map/ppermute | solution.py:322
  44.8 0.0 collective-permute-start.6
  44.8 2.8 %collective-permute-done.7.rest_2_ = f32[128,128]{1,0:T(8,128)S(1)} collective-permute-done((f32[128,128]{1,0:T(8,128)S(1)}, f32[128,128]{1,0:T(8,128)S(1)}, u32[]{:S(2)}, u32[]{:S(2)}) %collective-permute-start.7) | collective-permute-done | bytes 65568 | tf_op jit(solution)/shard_map/ppermute | solution.py:322
  47.6 0.0 collective-permute-start.8
  47.6 0.6 %copy.21 = f32[128,128]{1,0:T(8,128)} copy(f32[128,128]{1,0:T(8,128)S(1)} %value.1.rest_0_) | data formatting | bytes 131072
  48.2 0.0 collective-permute-done.6.rest_1_
  48.2 0.6 %collective-permute-done.8.rest_3_ = f32[128,128]{1,0:T(8,128)S(1)} collective-permute-done((f32[128,128]{1,0:T(8,128)S(1)}, f32[128,128]{1,0:T(8,128)S(1)}, u32[]{:S(2)}, u32[]{:S(2)}) %collective-permute-start.8) | collective-permute-done | bytes 65568 | tf_op jit(solution)/shard_map/ppermute | solution.py:322
  48.8 1.2 %lapse.1 = f32[1024,128]{1,0:T(8,128)} custom-call(bf16[1024,512]{1,0:T(8,128)(2,1)S(1)} %get-tuple-element.42.hot_ref, f32[1024,128]{1,0:T(8,128)S(1)} %get-tuple-element.43.level_ref, f32[128,128]{1,0:T(8,128)S(1)} %value.1.rest_0_, f32[128,128]{1,0:T(8,128)S(1)} %collective-permute-done.6.rest_1_, f32[128,128]{1,0:T(8,128)S(1)} %collective-permute-done.7.rest_2_, ...), custom_call_target="tpu_custom_call" | custom-call | tf_op jit(solution)/shard_map/lapse/pallas_call | solution.py:414
  (3 shorter events, 0.1 us)
Async XLA Ops:
  0.6 7.4 %collective-permute-start = (f32[1,8,2,128]{3,2,1,0:T(2,128)}, f32[1,8,2,128]{3,2,1,0:T(2,128)S(1)}, u32[]{:S(2)}, u32[]{:S(2)}) collective-permute-start(f32[1,8,2,128]{3,2,1,0:T(2,128)} %bitcast.17), channel_id=1, source_target_pairs={{0,1},{1,0},{2,3},{3,2},{4,5},{5,4},{6,7},{7,6},{8,9},{9,8},{10,11... | collective-permute-start | bytes 24584 | tf_op jit(solution)/shard_map/ppermute | solution.py:322
  3.7 4.3 %copy-start.3 = (f32[8,2,128]{2,1,0:T(2,128)S(1)}, f32[8,2,128]{2,1,0:T(2,128)}, u32[]{:S(2)}) copy-start(f32[8,2,128]{2,1,0:T(2,128)} %param.29) | copy-start | bytes 24580
  8.0 3.8 %collective-permute-start.1 = (f32[2,8,2,128]{3,2,1,0:T(2,128)S(1)}, f32[2,8,2,128]{3,2,1,0:T(2,128)S(1)}, u32[]{:S(2)}, u32[]{:S(2)}) collective-permute-start(f32[2,8,2,128]{3,2,1,0:T(2,128)S(1)} %pad_maximum_fusion.2), channel_id=1, source_target_pairs={{0,2},{1,3},{2,0},{3,1},{4,6},{5,7},{6,4},{7,5},{8,10},{9,11},{10,... | collective-permute-start | bytes 49160 | tf_op jit(solution)/shard_map/ppermute | solution.py:322
  9.7 7.5 %collective-permute-start.3 = (f32[392,128]{1,0:T(8,128)S(1)}, f32[392,128]{1,0:T(8,128)S(1)}, u32[]{:S(2)}, u32[]{:S(2)}) collective-permute-start(f32[392,128]{1,0:T(8,128)S(1)} %get-tuple-element.46), channel_id=1, source_target_pairs={{0,8},{8,0},{16,24},{24,16},{1,9},{9,1},{17,25},{25,17},{2,10},{10... | collective-permute-start | bytes 602120 | tf_op jit(solution)/shard_map/ppermute | solution.py:322
  9.7 7.9 %collective-permute-start.4 = (f32[392,128]{1,0:T(8,128)S(1)}, f32[392,128]{1,0:T(8,128)S(1)}, u32[]{:S(2)}, u32[]{:S(2)}) collective-permute-start(f32[392,128]{1,0:T(8,128)S(1)} %get-tuple-element.47), channel_id=1, source_target_pairs={{0,16},{8,24},{16,0},{24,8},{1,17},{9,25},{17,1},{25,9},{2,18},{10... | collective-permute-start | bytes 602120 | tf_op jit(solution)/shard_map/ppermute | solution.py:322
  11.2 9.7 %collective-permute-start.5 = (f32[392,128]{1,0:T(8,128)S(1)}, f32[392,128]{1,0:T(8,128)S(1)}, u32[]{:S(2)}, u32[]{:S(2)}) collective-permute-start(f32[392,128]{1,0:T(8,128)S(1)} %get-tuple-element.48), channel_id=1, source_target_pairs={{0,24},{8,16},{16,8},{24,0},{1,25},{9,17},{17,9},{25,1},{2,26},{10... | collective-permute-start | bytes 602120 | tf_op jit(solution)/shard_map/ppermute | solution.py:322
  11.9 3.3 %copy-start.1 = (s32[1024]{0:T(1024)S(1)}, s32[1024]{0:T(1024)}, u32[]{:S(2)}) copy-start(s32[1024]{0:T(1024)} %param.21) | copy-start | bytes 12292
  11.9 3.4 %copy-start.2 = (f32[10,16]{1,0:T(8,128)S(1)}, f32[10,16]{1,0:T(8,128)}, u32[]{:S(2)}) copy-start(f32[10,16]{1,0:T(8,128)} %base_ref.1) | copy-start | bytes 1924
  11.9 3.3 %copy-start = (s32[1024]{0:T(1024)S(1)}, s32[1024]{0:T(1024)}, u32[]{:S(2)}) copy-start(s32[1024]{0:T(1024)} %param.20) | copy-start | bytes 12292
  11.9 4.9 %collective-permute-start.2 = (f32[4,8,2,128]{3,2,1,0:T(2,128)S(1)}, f32[4,8,2,128]{3,2,1,0:T(2,128)S(1)}, u32[]{:S(2)}, u32[]{:S(2)}) collective-permute-start(f32[4,8,2,128]{3,2,1,0:T(2,128)S(1)} %pad_maximum_fusion.1), channel_id=1, source_target_pairs={{0,4},{1,5},{2,6},{3,7},{4,0},{5,1},{6,2},{7,3},{8,12},{9,13},{10,... | collective-permute-start | bytes 98312 | tf_op jit(solution)/shard_map/ppermute | solution.py:322
  43.3 4.3 %collective-permute-start.7 = (f32[128,128]{1,0:T(8,128)S(1)}, f32[128,128]{1,0:T(8,128)S(1)}, u32[]{:S(2)}, u32[]{:S(2)}) collective-permute-start(f32[128,128]{1,0:T(8,128)S(1)} %value.1.rest_0_), channel_id=1, source_target_pairs={{0,16},{8,24},{16,0},{24,8},{1,17},{9,25},{17,1},{25,9},{2,18},{10... | collective-permute-start | bytes 196616 | tf_op jit(solution)/shard_map/ppermute | solution.py:322
  44.8 3.4 %collective-permute-start.6 = (f32[128,128]{1,0:T(8,128)S(1)}, f32[128,128]{1,0:T(8,128)S(1)}, u32[]{:S(2)}, u32[]{:S(2)}) collective-permute-start(f32[128,128]{1,0:T(8,128)S(1)} %value.1.rest_0_), channel_id=1, source_target_pairs={{0,8},{8,0},{16,24},{24,16},{1,9},{9,1},{17,25},{25,17},{2,10},{10... | collective-permute-start | bytes 196616 | tf_op jit(solution)/shard_map/ppermute | solution.py:322
  47.6 1.3 %collective-permute-start.8 = (f32[128,128]{1,0:T(8,128)S(1)}, f32[128,128]{1,0:T(8,128)S(1)}, u32[]{:S(2)}, u32[]{:S(2)}) collective-permute-start(f32[128,128]{1,0:T(8,128)S(1)} %collective-permute-done.7.rest_2_), channel_id=1, source_target_pairs={{0,8},{8,0},{16,24},{24,16},{1,9},{9,1},{17,25},{25,17},{2,10},{10... | collective-permute-start | bytes 196616 | tf_op jit(solution)/shard_map/ppermute | solution.py:322

commit v2 on v1

--- a/solution.py
+++ b/solution.py
@@ -131,20 +131,24 @@
         column = jnp.broadcast_to(combo[:, b:b + 1], slot.shape)
         hot[b * LANES:(b + 1) * LANES, :] = onehot(column, slot)
 
-    for o in range(n_proj):
+    def arrange(o):
         mine = masks[o * blocks:(o + 1) * blocks] > 0.0
         rank = jnp.where(mine, before[o * blocks:(o + 1) * blocks], -1.0)
-        label = jnp.where(mine, local, -1.0)
+        for b in range(blocks):
+            move[o * rows:(o + 1) * rows, b * LANES:(b + 1) * LANES] = onehot(rank[b:b + 1], ramp[:rows, :])
+
+    for o in range(n_proj):
+        label = jnp.where(masks[o * blocks:(o + 1) * blocks] > 0.0, local, -1.0)
         for b in range(blocks):
             span = slice(b * LANES, (b + 1) * LANES)
-            move[o * rows:(o + 1) * rows, span] = onehot(rank[b:b + 1], ramp[:rows, :])
             gather[o * owned:(o + 1) * owned, span] = onehot(label[b:b + 1], ramp[:owned, :])
+    for o in range(n_proj // 2):
+        arrange(o)
     kind = product_ref[...].astype(F32)
     which = iota((16, LANES), 0)
     facts = jnp.concatenate(
         [jnp.where(which == 0, kind[b:b + 1], jnp.where(which == 1, local[b:b + 1], 0.0)) for b in range(blocks)],
         axis=1).astype(BF16)
-    told = lax.dot_general(facts, move[...], (((1,), (1,)), ((), ())), preferred_element_type=F32)
 
     for copy in loads:
         copy.wait()
@@ -160,16 +164,21 @@
         result[...] = value
     weighted[...] = halves(n * f)
     secured[...] = halves(n * g)
-    moved = join(dot(move[...], weighted[...]))
     summed = join(dot(gather[...], secured[...]))
-    for o in range(n_proj):
-        send = sends[o]
-        send[:rows, :] = moved[o * rows:(o + 1) * rows]
-        send[rows:rows + owned, :] = summed[o * owned:(o + 1) * owned]
-        for b in range(rows // LANES):
-            start = rows + owned + 2 * b
-            first = o * rows + b * LANES
-            send[start:start + 2, :] = told[:2, first:first + LANES]
+    for first in (0, n_proj // 2):
+        span = slice(first * rows, (first + n_proj // 2) * rows)
+        moved = join(dot(move[span, :], weighted[...]))
+        told = lax.dot_general(facts, move[span, :], (((1,), (1,)), ((), ())), preferred_element_type=F32)
+        for o in range(first, first + n_proj // 2):
+            if not first:
+                arrange(o + n_proj // 2)
+            send = sends[o]
+            at = (o - first) * rows
+            send[:rows, :] = moved[at:at + rows]
+            send[rows:rows + owned, :] = summed[o * owned:(o + 1) * owned]
+            for b in range(rows // LANES):
+                start = rows + owned + 2 * b
+                send[start:start + 2, :] = told[:2, at + b * LANES:at + (b + 1) * LANES]
 
 
 def hot_kernel(owned, year_ref, cohort_ref, product_ref, base_ref, *refs):
@@ -298,11 +307,22 @@
     lax.fori_loop(0, turns // 2, pair, 0)
 
 
-def lapse_kernel(n_proj, hot_ref, level_ref, *rest):
-    costs, (out_hbm, out, sem) = rest[:n_proj], rest[n_proj:]
-    factors = jnp.concatenate(
+def rates(costs):
+    return jnp.concatenate(
         [halves(LAPSE_FLOOR + LAPSE_SPAN * jax.nn.sigmoid(LAPSE_SLOPE * (LAPSE_PIVOT - cost[...]))) for cost in costs],
         axis=0)
+
+
+def near_kernel(hot_ref, *rest):
+    costs, out_ref = rest[:-1], rest[-1]
+    factors = rates(costs)
+    out_ref[...] = join(dot(hot_ref[:, :factors.shape[0]], factors))
+
+
+def lapse_kernel(hot_ref, near_ref, level_ref, *rest):
+    costs, (out_hbm, out, sem) = rest[:-3], rest[-3:]
+    factors = rates(costs)
+    first = hot_ref.shape[1] - factors.shape[0]
     chunk = 2 * LANES
 
     def flush(i):
@@ -312,7 +332,7 @@
     chunks = out.shape[0] // chunk
     for i in range(chunks):
         span = slice(i * chunk, (i + 1) * chunk)
-        out[span, :] = level_ref[span, :] * join(dot(hot_ref[span, :], factors))
+        out[span, :] = level_ref[span, :] * (near_ref[span, :] + join(dot(hot_ref[span, first:], factors)))
         flush(i).start()
     for i in range(chunks):
         flush(i).wait()
@@ -411,12 +431,17 @@
         near = o % 2 and o > 1
         costs.append(exchange(costs[o - 1] if near else cost, "proj", 1 if near else o))
     costs = [cost] + [vmem(x) for x in costs[1:]]
+    near = pl.pallas_call(
+        near_kernel,
+        out_shape=pltpu.VMEM((points, width), F32), in_specs=[VMEM] * 3, out_specs=VMEM,
+        compiler_params=limit(8), name="near",
+    )(hot, *costs[:2])
     lapse_next = pl.pallas_call(
-        functools.partial(lapse_kernel, n_proj),
-        out_shape=plane, in_specs=[VMEM] * (2 + n_proj), out_specs=HBM,
+        lapse_kernel,
+        out_shape=plane, in_specs=[VMEM] * (1 + n_proj), out_specs=HBM,
         scratch_shapes=[pltpu.VMEM((points, width), F32), pltpu.SemaphoreType.DMA((points // (2 * LANES),))],
         compiler_params=limit(16), name="lapse",
-    )(hot, level, *costs)
+    )(hot, near, level, *costs[2:])
     return fund_next, force_next, base_next, lapse_next, cost
 
 

time: 50.2 us -> 50 us (level)
    pallas_call x1 -> x2, Pallas kernels: 1.19 us -> 1.37 us  [the longest x1 1.07 us: body(): pl.pallas_call(lapse_kernel, out_shape=plane, in_specs=[VMEM] * (1 + n_pr...]
where the time goes in v2:
time: 50 us; the launch traced here: 49.8 us
  Pallas kernels  29.5 us (59%)
  starting transfers between devices  10.7 us (21%)
  waiting for transfers between devices  7.48 us (15%)
  between operations  1.4 us (3%)
  local copies, waits for them, and re-layouts  0.65 us (1%)
    pallas_call x1, Pallas kernels, body(): pl.pallas_call(functools.partial(value_kernel, (n_proj, owned, rows, hori...  22.3 us
    ppermute x9, starting transfers between devices, exchange(): return lax.ppermute(x, axis, flips(lax.axis_size(axis), offset))  10.7 us
    ppermute x9, waiting for transfers between devices, exchange(): return lax.ppermute(x, axis, flips(lax.axis_size(axis), offset))  7.48 us
    pallas_call x1, Pallas kernels, body(): pl.pallas_call(functools.partial(project_kernel, (n_proj, owned, rows)),...  4.23 us
    pallas_call x1, Pallas kernels, body(): pl.pallas_call(functools.partial(hot_kernel, owned), out_shape=[pltpu.VME...  1.26 us
    pallas_call x1, Pallas kernels, body(): pl.pallas_call(lapse_kernel, out_shape=plane, in_specs=[VMEM] * (1 + n_pr...  1.07 us
  transfers between devices with their start and end apart: 9, of which 6 were waited for; matrix products, arithmetic and copies ran while one was open for 1% of the time, Pallas kernels for 12%

profile of v2, /device:TPU:0, one launch (start us, length us, event | category | flops | bytes accessed | tf_op | source)
XLA Modules:
  0.0 49.8 jit_solution(15246855321450540453)
XLA Ops:
  0.6 3.1 %collective-permute-start = (f32[1,8,2,128]{3,2,1,0:T(2,128)}, f32[1,8,2,128]{3,2,1,0:T(2,128)S(1)}, u32[]{:S(2)}, u32[]{:S(2)}) collective-permute-start(f32[1,8,2,128]{3,2,1,0:T(2,128)} %bitcast.17), channel_id=1, source_target_pairs={{0,1},{1,0},{2,3},{3,2},{4,5},{5,4},{6,7},{7,6},{8,9},{9,8},{10,11... | collective-permute-start | bytes 24584 | tf_op jit(solution)/shard_map/ppermute | solution.py:342
  3.7 0.0 copy-start.3
  3.7 4.2 %project.1 = (f32[392,128]{1,0:T(8,128)S(1)}, f32[392,128]{1,0:T(8,128)S(1)}, f32[392,128]{1,0:T(8,128)S(1)}, f32[392,128]{1,0:T(8,128)S(1)}, f32[1024,128]{1,0:...) custom-call(s32[8,128]{1,0:T(8,128)} %bitcast.10, s32[8,128]{1,0:T(8,128)} %bitcast.12, ...), custom_call_target="tpu_custom_call" | custom-call | tf_op jit(solution)/shard_map/project/pallas_call | solution.py:369
  7.9 0.0 collective-permute-done
  7.9 0.0 copy-done.3
  8.0 1.6 %collective-permute-start.1 = (f32[2,8,2,128]{3,2,1,0:T(2,128)S(1)}, f32[2,8,2,128]{3,2,1,0:T(2,128)S(1)}, u32[]{:S(2)}, u32[]{:S(2)}) collective-permute-start(f32[2,8,2,128]{3,2,1,0:T(2,128)S(1)} %pad_maximum_fusion.2), channel_id=1, source_target_pairs={{0,2},{1,3},{2,0},{3,1},{4,6},{5,7},{6,4},{7,5},{8,10},{9,11},{10,... | collective-permute-start | bytes 49160 | tf_op jit(solution)/shard_map/ppermute | solution.py:342
  9.6 0.0 collective-permute-start.3
  9.6 1.5 %collective-permute-start.4 = (f32[392,128]{1,0:T(8,128)S(1)}, f32[392,128]{1,0:T(8,128)S(1)}, u32[]{:S(2)}, u32[]{:S(2)}) collective-permute-start(f32[392,128]{1,0:T(8,128)S(1)} %get-tuple-element.46), channel_id=1, source_target_pairs={{0,16},{8,24},{16,0},{24,8},{1,17},{9,25},{17,1},{25,9},{2,18},{10... | collective-permute-start | bytes 602120 | tf_op jit(solution)/shard_map/ppermute | solution.py:342
  11.1 0.4 collective-permute-start.5
  11.5 0.3 collective-permute-done.1
  11.8 0.0 copy-start.1
  11.8 0.0 copy-start
  11.8 2.6 %collective-permute-start.2 = (f32[4,8,2,128]{3,2,1,0:T(2,128)S(1)}, f32[4,8,2,128]{3,2,1,0:T(2,128)S(1)}, u32[]{:S(2)}, u32[]{:S(2)}) collective-permute-start(f32[4,8,2,128]{3,2,1,0:T(2,128)S(1)} %pad_maximum_fusion.1), channel_id=1, source_target_pairs={{0,4},{1,5},{2,6},{3,7},{4,0},{5,1},{6,2},{7,3},{8,12},{9,13},{10,... | collective-permute-start | bytes 98312 | tf_op jit(solution)/shard_map/ppermute | solution.py:342
  15.1 0.0 copy-done.1
  15.1 0.0 copy-done.2
  15.1 0.0 copy-done
  15.1 1.3 %cohort_hot.1 = (bf16[1024,512]{1,0:T(8,128)(2,1)S(1)}, f32[1024,128]{1,0:T(8,128)S(1)}, f32[1024,128]{1,0:T(8,128)}, f32[1024,128]{1,0:T(8,128)}, f32[1024,128]{1,0:T(8,128)}) custom-call(s32[1]{0:T(128)S(6)} %copy.22.year_ref, s32[8,128]{1,0:T(8,128)S(1)} %bitcast.11, s32[8,128]{1,0:T(8,128)S(1)} %bitcast.13, f32[10,16]{1,0:T(8,128)S(1)} %copy-done.2, ...), custom_call_target="tpu_custom_call" | custom-call | tf_op jit(solution)/shard_map/cohort_hot/pallas_call | solution.py:400
  16.4 0.3 collective-permute-done.2
  16.7 0.4 paths.1.paths_ref
  17.1 0.0 collective-permute-done.3.rest_1_
  17.1 0.4 collective-permute-done.4.rest_2_
  17.5 3.4 %collective-permute-done.5.rest_3_ = f32[392,128]{1,0:T(8,128)S(1)} collective-permute-done((f32[392,128]{1,0:T(8,128)S(1)}, f32[392,128]{1,0:T(8,128)S(1)}, u32[]{:S(2)}, u32[]{:S(2)}) %collective-permute-start.5) | collective-permute-done | bytes 200736 | tf_op jit(solution)/shard_map/ppermute | solution.py:342
  20.8 22.3 %value.1.rest_0_ = f32[128,128]{1,0:T(8,128)S(1)} custom-call(f32[1,8]{1,0:T(1,128)} %bitcast.20, f32[1,128]{1,0:T(1,128)} %bitcast.21, f32[8,16]{1,0:T(8,128)} %bitcast.16, bf16[2048,64]{1,0:T(8,128)(2,1)S(1)} %paths.1.paths_ref, f32[392,128]{1,0:T(8,128)S(1)} %get-tuple-element.44.rest_0_, f32[392,128]{1,0:T(8,128)S(1)} %collective-permute-done.3.rest_1_, ...), custom_call_target="tpu_custom_call" | custom-call | tf_op jit(solution)/shard_map/value/pallas_call | solution.py:415
  43.2 1.5 %collective-permute-start.7 = (f32[128,128]{1,0:T(8,128)S(1)}, f32[128,128]{1,0:T(8,128)S(1)}, u32[]{:S(2)}, u32[]{:S(2)}) collective-permute-start(f32[128,128]{1,0:T(8,128)S(1)} %value.1.rest_0_), channel_id=1, source_target_pairs={{0,16},{8,24},{16,0},{24,8},{1,17},{9,25},{17,1},{25,9},{2,18},{10... | collective-permute-start | bytes 196616 | tf_op jit(solution)/shard_map/ppermute | solution.py:342
  44.7 0.0 collective-permute-start.6
  44.7 2.8 %collective-permute-done.7.rest_0_ = f32[128,128]{1,0:T(8,128)S(1)} collective-permute-done((f32[128,128]{1,0:T(8,128)S(1)}, f32[128,128]{1,0:T(8,128)S(1)}, u32[]{:S(2)}, u32[]{:S(2)}) %collective-permute-start.7) | collective-permute-done | bytes 65568 | tf_op jit(solution)/shard_map/ppermute | solution.py:342
  47.5 0.0 collective-permute-start.8
  47.5 0.6 %copy.21 = f32[128,128]{1,0:T(8,128)} copy(f32[128,128]{1,0:T(8,128)S(1)} %value.1.rest_0_) | data formatting | bytes 131072
  48.2 0.0 collective-permute-done.6.rest_1_
  48.2 0.3 near.1.near_ref
  48.5 0.3 collective-permute-done.8.rest_1_
  48.8 1.1 %lapse.1 = f32[1024,128]{1,0:T(8,128)} custom-call(bf16[1024,512]{1,0:T(8,128)(2,1)S(1)} %get-tuple-element.42.hot_ref, f32[1024,128]{1,0:T(8,128)S(1)} %near.1.near_ref, f32[1024,128]{1,0:T(8,128)S(1)} %get-tuple-element.48.level_ref, f32[128,128]{1,0:T(8,128)S(1)} %collective-permute-done.7.rest_0_, f32[128,128]{1,0:T(8,128)S(1)} %collective-permute-done.8.rest_1_), custom_call_target="tpu_custom_call" | custom-call | tf_op jit(solution)/shard_map/lapse/pallas_call | solution.py:439
  (4 shorter events, 0.1 us)
Async XLA Ops:
  0.6 7.3 %collective-permute-start = (f32[1,8,2,128]{3,2,1,0:T(2,128)}, f32[1,8,2,128]{3,2,1,0:T(2,128)S(1)}, u32[]{:S(2)}, u32[]{:S(2)}) collective-permute-start(f32[1,8,2,128]{3,2,1,0:T(2,128)} %bitcast.17), channel_id=1, source_target_pairs={{0,1},{1,0},{2,3},{3,2},{4,5},{5,4},{6,7},{7,6},{8,9},{9,8},{10,11... | collective-permute-start | bytes 24584 | tf_op jit(solution)/shard_map/ppermute | solution.py:342
  3.7 4.2 %copy-start.3 = (f32[8,2,128]{2,1,0:T(2,128)S(1)}, f32[8,2,128]{2,1,0:T(2,128)}, u32[]{:S(2)}) copy-start(f32[8,2,128]{2,1,0:T(2,128)} %param.29) | copy-start | bytes 24580
  8.0 3.8 %collective-permute-start.1 = (f32[2,8,2,128]{3,2,1,0:T(2,128)S(1)}, f32[2,8,2,128]{3,2,1,0:T(2,128)S(1)}, u32[]{:S(2)}, u32[]{:S(2)}) collective-permute-start(f32[2,8,2,128]{3,2,1,0:T(2,128)S(1)} %pad_maximum_fusion.2), channel_id=1, source_target_pairs={{0,2},{1,3},{2,0},{3,1},{4,6},{5,7},{6,4},{7,5},{8,10},{9,11},{10,... | collective-permute-start | bytes 49160 | tf_op jit(solution)/shard_map/ppermute | solution.py:342
  9.6 7.5 %collective-permute-start.3 = (f32[392,128]{1,0:T(8,128)S(1)}, f32[392,128]{1,0:T(8,128)S(1)}, u32[]{:S(2)}, u32[]{:S(2)}) collective-permute-start(f32[392,128]{1,0:T(8,128)S(1)} %get-tuple-element.45), channel_id=1, source_target_pairs={{0,8},{8,0},{16,24},{24,16},{1,9},{9,1},{17,25},{25,17},{2,10},{10... | collective-permute-start | bytes 602120 | tf_op jit(solution)/shard_map/ppermute | solution.py:342
  9.6 7.9 %collective-permute-start.4 = (f32[392,128]{1,0:T(8,128)S(1)}, f32[392,128]{1,0:T(8,128)S(1)}, u32[]{:S(2)}, u32[]{:S(2)}) collective-permute-start(f32[392,128]{1,0:T(8,128)S(1)} %get-tuple-element.46), channel_id=1, source_target_pairs={{0,16},{8,24},{16,0},{24,8},{1,17},{9,25},{17,1},{25,9},{2,18},{10... | collective-permute-start | bytes 602120 | tf_op jit(solution)/shard_map/ppermute | solution.py:342
  11.1 9.8 %collective-permute-start.5 = (f32[392,128]{1,0:T(8,128)S(1)}, f32[392,128]{1,0:T(8,128)S(1)}, u32[]{:S(2)}, u32[]{:S(2)}) collective-permute-start(f32[392,128]{1,0:T(8,128)S(1)} %get-tuple-element.47), channel_id=1, source_target_pairs={{0,24},{8,16},{16,8},{24,0},{1,25},{9,17},{17,9},{25,1},{2,26},{10... | collective-permute-start | bytes 602120 | tf_op jit(solution)/shard_map/ppermute | solution.py:342
  11.8 3.3 %copy-start.1 = (s32[1024]{0:T(1024)S(1)}, s32[1024]{0:T(1024)}, u32[]{:S(2)}) copy-start(s32[1024]{0:T(1024)} %param.21) | copy-start | bytes 12292
  11.8 3.3 %copy-start.2 = (f32[10,16]{1,0:T(8,128)S(1)}, f32[10,16]{1,0:T(8,128)}, u32[]{:S(2)}) copy-start(f32[10,16]{1,0:T(8,128)} %base_ref.1) | copy-start | bytes 1924
  11.8 3.3 %copy-start = (s32[1024]{0:T(1024)S(1)}, s32[1024]{0:T(1024)}, u32[]{:S(2)}) copy-start(s32[1024]{0:T(1024)} %param.20) | copy-start | bytes 12292
  11.8 4.9 %collective-permute-start.2 = (f32[4,8,2,128]{3,2,1,0:T(2,128)S(1)}, f32[4,8,2,128]{3,2,1,0:T(2,128)S(1)}, u32[]{:S(2)}, u32[]{:S(2)}) collective-permute-start(f32[4,8,2,128]{3,2,1,0:T(2,128)S(1)} %pad_maximum_fusion.1), channel_id=1, source_target_pairs={{0,4},{1,5},{2,6},{3,7},{4,0},{5,1},{6,2},{7,3},{8,12},{9,13},{10,... | collective-permute-start | bytes 98312 | tf_op jit(solution)/shard_map/ppermute | solution.py:342
  43.2 4.4 %collective-permute-start.7 = (f32[128,128]{1,0:T(8,128)S(1)}, f32[128,128]{1,0:T(8,128)S(1)}, u32[]{:S(2)}, u32[]{:S(2)}) collective-permute-start(f32[128,128]{1,0:T(8,128)S(1)} %value.1.rest_0_), channel_id=1, source_target_pairs={{0,16},{8,24},{16,0},{24,8},{1,17},{9,25},{17,1},{25,9},{2,18},{10... | collective-permute-start | bytes 196616 | tf_op jit(solution)/shard_map/ppermute | solution.py:342
  44.7 3.4 %collective-permute-start.6 = (f32[128,128]{1,0:T(8,128)S(1)}, f32[128,128]{1,0:T(8,128)S(1)}, u32[]{:S(2)}, u32[]{:S(2)}) collective-permute-start(f32[128,128]{1,0:T(8,128)S(1)} %value.1.rest_0_), channel_id=1, source_target_pairs={{0,8},{8,0},{16,24},{24,16},{1,9},{9,1},{17,25},{25,17},{2,10},{10... | collective-permute-start | bytes 196616 | tf_op jit(solution)/shard_map/ppermute | solution.py:342
  47.5 1.3 %collective-permute-start.8 = (f32[128,128]{1,0:T(8,128)S(1)}, f32[128,128]{1,0:T(8,128)S(1)}, u32[]{:S(2)}, u32[]{:S(2)}) collective-permute-start(f32[128,128]{1,0:T(8,128)S(1)} %collective-permute-done.7.rest_0_), channel_id=1, source_target_pairs={{0,8},{8,0},{16,24},{24,16},{1,9},{9,1},{17,25},{25,17},{2,10},{10... | collective-permute-start | bytes 196616 | tf_op jit(solution)/shard_map/ppermute | solution.py:342

commit v3 on v2

--- a/solution.py
+++ b/solution.py
@@ -181,24 +181,29 @@
                 send[start:start + 2, :] = told[:2, at + b * LANES:at + (b + 1) * LANES]
 
 
-def hot_kernel(owned, year_ref, cohort_ref, product_ref, base_ref, *refs):
-    planes, (hot_ref, level_ref), results, sem = refs[:3], refs[3:5], refs[5:8], refs[8]
+def hot_kernel(owned, cohort_ref, *refs):
+    planes, hot_ref, results, sem = refs[:3], refs[3], refs[4:7], refs[7]
     stores = [pltpu.make_async_copy(planes[i], results[i], sem.at[i]) for i in range(3)]
     for copy in stores:
         copy.start()
     _, label = relabel(cohort_ref[...], owned, lax.axis_index("proj"))
     label = label.astype(F32).T
-    product = product_ref[...].astype(F32).T
     slot = iota((LANES, hot_ref.shape[1]), 1).astype(F32)
-    rates = base_ref[pl.ds(year_ref[0], 1), :]
     for b in range(hot_ref.shape[0] // LANES):
-        span = slice(b * LANES, (b + 1) * LANES)
-        hot_ref[span, :] = onehot(jnp.broadcast_to(label[:, b:b + 1], slot.shape), slot)
-        kind = jnp.broadcast_to(product[:, b:b + 1], (LANES, rates.shape[1]))
-        rate = jnp.sum(jnp.where(kind == slot[:, :rates.shape[1]], rates, 0.0), axis=1, keepdims=True)
-        level_ref[span, :] = jnp.broadcast_to(rate, (LANES, LANES))
+        hot_ref[b * LANES:(b + 1) * LANES, :] = onehot(jnp.broadcast_to(label[:, b:b + 1], slot.shape), slot)
     for copy in stores:
         copy.wait()
+
+
+def level_kernel(year_ref, product_ref, base_ref, level_ref):
+    product = product_ref[...].astype(F32).T
+    rates = base_ref[pl.ds(year_ref[0], 1), :]
+    shape = (LANES, rates.shape[1])
+    slot = iota(shape, 1).astype(F32)
+    for b in range(level_ref.shape[0] // LANES):
+        kind = jnp.broadcast_to(product[:, b:b + 1], shape)
+        rate = jnp.sum(jnp.where(kind == slot, rates, 0.0), axis=1, keepdims=True)
+        level_ref[b * LANES:(b + 1) * LANES, :] = jnp.broadcast_to(rate, (LANES, LANES))
 
 
 def paths_kernel(shocks_ref, paths_ref):
@@ -216,12 +221,13 @@
             paths_ref[start:start + width, :] = full.T.astype(BF16)
 
 
-def value_kernel(dims, vol_ref, sigma_ref, mix_ref, paths_ref, *rest):
+def value_kernel(dims, vol_ref, sigma_ref, mix_ref, early_ref, late_ref, *rest):
     n_proj, owned, rows, horizon, group, step = dims
     received = rest[:n_proj]
     cost_ref, weighted, mixes, loads, spare, money = rest[n_proj:]
     funds, products = mix_ref.shape
-    trials = paths_ref.shape[0] // horizon
+    half = early_ref.shape[0] // horizon
+    trials = 2 * half
     per = rows // LANES
     mix = mix_ref[...]
     mix = mix / jnp.sum(mix, axis=0, keepdims=True)
@@ -284,10 +290,11 @@
         total = None
         for h in range(horizon):
             reach = jnp.zeros((8, group * LANES), F32)
-            for s in range(trials // step):
-                left = paths_ref[h * trials + s * step:h * trials + (s + 1) * step, :]
-                kept = jnp.exp2(jnp.minimum(dot(left, right), 0.0))
-                reach = reach + jnp.sum(kept.reshape(step // 8, 8, group * LANES), axis=0)
+            for paths_ref in (early_ref, late_ref):
+                for s in range(half // step):
+                    left = paths_ref[h * half + s * step:h * half + (s + 1) * step, :]
+                    kept = jnp.exp2(jnp.minimum(dot(left, right), 0.0))
+                    reach = reach + jnp.sum(kept.reshape(step // 8, 8, group * LANES), axis=0)
             part = (float(trials) - jnp.sum(reach, axis=0, keepdims=True)) * (DISCOUNT ** (h + 1) / trials)
             total = part if total is None else total + part
         for c in range(group):
@@ -392,30 +399,39 @@
     offset = 2
     while offset < n_scen:
         if 2 * offset >= n_scen:
-            sheets, labels, year_index = lax.optimization_barrier((sheets, labels, year_index))
-        sheets = jnp.concatenate([sheets, exchange(sheets, "scen", offset)], axis=0)
+            sheets, kinds, year_index = lax.optimization_barrier((sheets, kinds, year_index))
+        late = exchange(sheets, "scen", offset)
+        if 2 * offset < n_scen:
+            sheets = jnp.concatenate([sheets, late], axis=0)
         offset *= 2
     trials = n_scen * shocks.shape[2]
 
-    hot, level, fund_next, force_next, base_next = pl.pallas_call(
+    build = pl.pallas_call(
         functools.partial(hot_kernel, owned),
-        out_shape=[pltpu.VMEM((points, COHORTS), BF16), pltpu.VMEM((points, width), F32)] + [plane] * 3,
-        in_specs=[pl.BlockSpec(memory_space=pltpu.SMEM)] + [VMEM] * 6, out_specs=[VMEM] * 2 + [HBM] * 3,
+        out_shape=[pltpu.VMEM((points, COHORTS), BF16)] + [plane] * 3,
+        in_specs=[VMEM] * 4, out_specs=[VMEM] + [HBM] * 3,
         scratch_shapes=[pltpu.SemaphoreType.DMA((3,))],
         compiler_params=limit(8), name="cohort_hot",
-    )(year_index, labels, kinds, base_table, *planes)
-    left = pl.pallas_call(
+    )
+    hot, fund_next, force_next, base_next = build(hbm(labels), *planes)
+    level = pl.pallas_call(
+        level_kernel,
+        out_shape=pltpu.VMEM((points, width), F32),
+        in_specs=[pl.BlockSpec(memory_space=pltpu.SMEM)] + [VMEM] * 2, out_specs=VMEM,
+        compiler_params=limit(8), name="level",
+    )(year_index, hbm(kinds), hbm(base_table))
+    halved = [pl.pallas_call(
         paths_kernel,
-        out_shape=pltpu.VMEM((horizon * trials, DEPTH), BF16),
+        out_shape=pltpu.VMEM((horizon * trials // 2, DEPTH), BF16),
         in_specs=[VMEM], out_specs=VMEM, compiler_params=limit(8), name="paths",
-    )(vmem(sheets))
-    left, hot = lax.optimization_barrier((left, hot))
+    )(vmem(x)) for x in (sheets, late)]
+    late, level = lax.optimization_barrier((halved[1], level))
 
     group = 16
     cost = pl.pallas_call(
         functools.partial(value_kernel, (n_proj, owned, rows, horizon, group, 64)),
         out_shape=pltpu.VMEM((owned, width), F32),
-        in_specs=[VMEM] * (4 + n_proj), out_specs=VMEM,
+        in_specs=[VMEM] * (5 + n_proj), out_specs=VMEM,
         scratch_shapes=[
             pltpu.VMEM((n_proj * rows, 2 * width), BF16),
             pltpu.VMEM((2, n_proj * rows // LANES, funds, LANES), F32),
@@ -424,7 +440,7 @@
             pltpu.VMEM((owned, width), F32),
         ],
         compiler_params=limit(24), name="value",
-    )(hbm(fund_vol.reshape(1, funds)), hbm(closing_sigma_figure.reshape(1, width)), hbm(mix), left, *received)
+    )(hbm(fund_vol.reshape(1, funds)), hbm(closing_sigma_figure.reshape(1, width)), hbm(mix), halved[0], late, *received)
 
     costs = [cost]
     for o in range(1, n_proj):

time: 50 us -> 50.2 us (level)
  waiting for transfers between devices: 7.48 us -> 5.12 us
  Pallas kernels: 29.5 us -> 31.8 us
    ppermute x9, waiting for transfers between devices: 7.48 us -> 5.12 us  [exchange(): return lax.ppermute(x, axis, flips(lax.axis_size(axis), offset))]
    pallas_call x2 -> x4, Pallas kernels: 1.61 us -> 3.87 us  [the longest x1 1.85 us: body(): hot, fund_next, force_next, base_next = build(hbm(labels), *planes)]
  transfers between devices with their start and end apart: 9 -> 9, of which waited for: 6 -> 3; matrix products, arithmetic and copies ran while one was open for 1% -> 1% of each run, Pallas kernels for 12% -> 17%
where the time goes in v3:
time: 50.2 us; the launch traced here: 49.8 us
  Pallas kernels  31.8 us (63%)
  starting transfers between devices  10.9 us (22%)
  waiting for transfers between devices  5.12 us (10%)
  between operations  1.4 us (3%)
  local copies, waits for them, and re-layouts  0.64 us (1%)
    pallas_call x1, Pallas kernels, body(): pl.pallas_call(functools.partial(value_kernel, (n_proj, owned, rows, hori...  22.3 us
    ppermute x9, starting transfers between devices, exchange(): return lax.ppermute(x, axis, flips(lax.axis_size(axis), offset))  10.9 us
    ppermute x9, waiting for transfers between devices, exchange(): return lax.ppermute(x, axis, flips(lax.axis_size(axis), offset))  5.12 us
    pallas_call x1, Pallas kernels, body(): pl.pallas_call(functools.partial(project_kernel, (n_proj, owned, rows)),...  4.21 us
    pallas_call x1, Pallas kernels, body(): hot, fund_next, force_next, base_next = build(hbm(labels), *planes)  1.85 us
    pallas_call x1, Pallas kernels, body(): pl.pallas_call(level_kernel, out_shape=pltpu.VMEM((points, width), F32),...  1.59 us
    pallas_call x1, Pallas kernels, body(): pl.pallas_call(lapse_kernel, out_shape=plane, in_specs=[VMEM] * (1 + n_pr...  1.07 us
  transfers between devices with their start and end apart: 9, of which 3 were waited for; matrix products, arithmetic and copies ran while one was open for 1% of the time, Pallas kernels for 17%

profile of v3, /device:TPU:0, one launch (start us, length us, event | category | flops | bytes accessed | tf_op | source)
XLA Modules:
  0.0 49.8 jit_solution(3921233658549277278)
XLA Ops:
  0.6 3.1 %collective-permute-start = (f32[1,8,2,128]{3,2,1,0:T(2,128)}, f32[1,8,2,128]{3,2,1,0:T(2,128)S(1)}, u32[]{:S(2)}, u32[]{:S(2)}) collective-permute-start(f32[1,8,2,128]{3,2,1,0:T(2,128)} %bitcast.17), channel_id=1, source_target_pairs={{0,1},{1,0},{2,3},{3,2},{4,5},{5,4},{6,7},{7,6},{8,9},{9,8},{10,11... | collective-permute-start | bytes 24584 | tf_op jit(solution)/shard_map/ppermute | solution.py:349
  3.7 0.0 copy-start
  3.7 4.2 %project.1 = (f32[392,128]{1,0:T(8,128)S(1)}, f32[392,128]{1,0:T(8,128)S(1)}, f32[392,128]{1,0:T(8,128)S(1)}, f32[392,128]{1,0:T(8,128)S(1)}, f32[1024,128]{1,0:...) custom-call(s32[8,128]{1,0:T(8,128)} %bitcast.15, s32[8,128]{1,0:T(8,128)} %bitcast.11, ...), custom_call_target="tpu_custom_call" | custom-call | tf_op jit(solution)/shard_map/project/pallas_call | solution.py:376
  7.9 0.0 collective-permute-done
  7.9 0.0 copy-done
  8.0 0.1 collective-permute-start.3
  8.0 1.6 %collective-permute-start.4 = (f32[392,128]{1,0:T(8,128)S(1)}, f32[392,128]{1,0:T(8,128)S(1)}, u32[]{:S(2)}, u32[]{:S(2)}) collective-permute-start(f32[392,128]{1,0:T(8,128)S(1)} %get-tuple-element.44), channel_id=1, source_target_pairs={{0,16},{8,24},{16,0},{24,8},{1,17},{9,25},{17,1},{25,9},{2,18},{10... | collective-permute-start | bytes 602120 | tf_op jit(solution)/shard_map/ppermute | solution.py:349
  9.6 0.3 collective-permute-start.5
  9.9 1.6 %collective-permute-start.1 = (f32[2,8,2,128]{3,2,1,0:T(2,128)S(1)}, f32[2,8,2,128]{3,2,1,0:T(2,128)S(1)}, u32[]{:S(2)}, u32[]{:S(2)}) collective-permute-start(f32[2,8,2,128]{3,2,1,0:T(2,128)S(1)} %pad_maximum_fusion.1), channel_id=1, source_target_pairs={{0,2},{1,3},{2,0},{3,1},{4,6},{5,7},{6,4},{7,5},{8,10},{9,11},{10,... | collective-permute-start | bytes 49160 | tf_op jit(solution)/shard_map/ppermute | solution.py:349
  11.5 2.2 %collective-permute-done.1 = f32[2,8,2,128]{3,2,1,0:T(2,128)S(1)} collective-permute-done((f32[2,8,2,128]{3,2,1,0:T(2,128)S(1)}, f32[2,8,2,128]{3,2,1,0:T(2,128)S(1)}, u32[]{:S(2)}, u32[]{:S(2)}) %collective-permute-start.1) | collective-permute-done | bytes 16416 | tf_op jit(solution)/shard_map/ppermute | solution.py:349
  13.6 2.7 %collective-permute-start.2 = (f32[4,8,2,128]{3,2,1,0:T(2,128)S(1)}, f32[4,8,2,128]{3,2,1,0:T(2,128)S(1)}, u32[]{:S(2)}, u32[]{:S(2)}) collective-permute-start(f32[4,8,2,128]{3,2,1,0:T(2,128)S(1)} %pad_maximum_fusion.shocks_ref), channel_id=1, source_target_pairs={{0,4},{1,5},{2,6},{3,7},{4,0},{5,1},{6,2},{7,3},{8,12},{9,13},{10,... | collective-permute-start | bytes 98312 | tf_op jit(solution)/shard_map/ppermute | solution.py:349
  17.0 0.2 paths.2.early_ref
  17.2 1.6 %level.1.level_ref = f32[1024,128]{1,0:T(8,128)S(1)} custom-call(s32[1]{0:T(128)S(6)} %copy.22.year_ref, s32[8,128]{1,0:T(8,128)} %bitcast.12, f32[10,16]{1,0:T(8,128)} %base_ref.1), custom_call_target="tpu_custom_call" | custom-call | tf_op jit(solution)/shard_map/level/pallas_call | solution.py:417
  18.8 0.0 collective-permute-done.2.shocks_ref
  18.8 0.2 paths.3.late_ref
  19.0 0.0 collective-permute-done.3.rest_1_
  19.0 0.0 collective-permute-done.4.rest_2_
  19.0 0.2 collective-permute-done.5.rest_3_
  19.2 22.3 %value.1.rest_0_ = f32[128,128]{1,0:T(8,128)S(1)} custom-call(f32[1,8]{1,0:T(1,128)} %bitcast.20, f32[1,128]{1,0:T(1,128)} %bitcast.21, f32[8,16]{1,0:T(8,128)} %bitcast.14, bf16[1024,64]{1,0:T(8,128)(2,1)S(1)} %paths.2.early_ref, bf16[1024,64]{1,0:T(8,128)(2,1)S(1)} %paths.3.late_ref, f32[392,128]{1,0:T(8,128)S(1)} %get-tuple-element.42.rest_0_, ...), custom_call_target="tpu_custom_call" | custom-call | tf_op jit(solution)/shard_map/value/pallas_call | solution.py:431
  41.5 1.6 %collective-permute-start.7 = (f32[128,128]{1,0:T(8,128)S(1)}, f32[128,128]{1,0:T(8,128)S(1)}, u32[]{:S(2)}, u32[]{:S(2)}) collective-permute-start(f32[128,128]{1,0:T(8,128)S(1)} %value.1.rest_0_), channel_id=1, source_target_pairs={{0,16},{8,24},{16,0},{24,8},{1,17},{9,25},{17,1},{25,9},{2,18},{10... | collective-permute-start | bytes 196616 | tf_op jit(solution)/shard_map/ppermute | solution.py:349
  43.1 0.1 collective-permute-start.6
  43.1 2.8 %collective-permute-done.7.rest_0_ = f32[128,128]{1,0:T(8,128)S(1)} collective-permute-done((f32[128,128]{1,0:T(8,128)S(1)}, f32[128,128]{1,0:T(8,128)S(1)}, u32[]{:S(2)}, u32[]{:S(2)}) %collective-permute-start.7) | collective-permute-done | bytes 65568 | tf_op jit(solution)/shard_map/ppermute | solution.py:349
  45.9 0.0 collective-permute-start.8
  45.9 1.9 %cohort_hot.1 = (bf16[1024,512]{1,0:T(8,128)(2,1)S(1)}, f32[1024,128]{1,0:T(8,128)}, f32[1024,128]{1,0:T(8,128)}, f32[1024,128]{1,0:T(8,128)}) custom-call(s32[8,128]{1,0:T(8,128)} %bitcast.16, f32[1024,128]{1,0:T(8,128)S(1)} %get-tuple-element.26.refs_0_, f32[1024,128]{1,0:T(8,128)S(1)} %get-tuple-element.27.refs_1_, f32[1024,128]{1,0:T(8,128)S(1)} %get-tuple-element.28.refs_2_), custom_call_target="tpu_custom_call" | custom-call | tf_op jit(solution)/shard_map/cohort_hot/pallas_call | solution.py:416
  47.8 0.6 %copy.21 = f32[128,128]{1,0:T(8,128)} copy(f32[128,128]{1,0:T(8,128)S(1)} %value.1.rest_0_) | data formatting | bytes 131072
  48.4 0.0 collective-permute-done.6.rest_1_
  48.4 0.3 near.1.near_ref
  48.7 0.0 collective-permute-done.8.rest_1_
  48.7 1.1 %lapse.1 = f32[1024,128]{1,0:T(8,128)} custom-call(bf16[1024,512]{1,0:T(8,128)(2,1)S(1)} %get-tuple-element.32.hot_ref, f32[1024,128]{1,0:T(8,128)S(1)} %near.1.near_ref, f32[1024,128]{1,0:T(8,128)S(1)} %level.1.level_ref, f32[128,128]{1,0:T(8,128)S(1)} %collective-permute-done.7.rest_0_, f32[128,128]{1,0:T(8,128)S(1)} %collective-permute-done.8.rest_1_), custom_call_target="tpu_custom_call" | custom-call | tf_op jit(solution)/shard_map/lapse/pallas_call | solution.py:455
  (2 shorter events, 0.0 us)
Async XLA Ops:
  0.6 7.3 %collective-permute-start = (f32[1,8,2,128]{3,2,1,0:T(2,128)}, f32[1,8,2,128]{3,2,1,0:T(2,128)S(1)}, u32[]{:S(2)}, u32[]{:S(2)}) collective-permute-start(f32[1,8,2,128]{3,2,1,0:T(2,128)} %bitcast.17), channel_id=1, source_target_pairs={{0,1},{1,0},{2,3},{3,2},{4,5},{5,4},{6,7},{7,6},{8,9},{9,8},{10,11... | collective-permute-start | bytes 24584 | tf_op jit(solution)/shard_map/ppermute | solution.py:349
  3.7 4.2 %copy-start = (f32[8,2,128]{2,1,0:T(2,128)S(1)}, f32[8,2,128]{2,1,0:T(2,128)}, u32[]{:S(2)}) copy-start(f32[8,2,128]{2,1,0:T(2,128)} %param.29) | copy-start | bytes 24580
  8.0 11.0 %collective-permute-start.3 = (f32[392,128]{1,0:T(8,128)S(1)}, f32[392,128]{1,0:T(8,128)S(1)}, u32[]{:S(2)}, u32[]{:S(2)}) collective-permute-start(f32[392,128]{1,0:T(8,128)S(1)} %get-tuple-element.43), channel_id=1, source_target_pairs={{0,8},{8,0},{16,24},{24,16},{1,9},{9,1},{17,25},{25,17},{2,10},{10... | collective-permute-start | bytes 602120 | tf_op jit(solution)/shard_map/ppermute | solution.py:349
  8.0 11.0 %collective-permute-start.4 = (f32[392,128]{1,0:T(8,128)S(1)}, f32[392,128]{1,0:T(8,128)S(1)}, u32[]{:S(2)}, u32[]{:S(2)}) collective-permute-start(f32[392,128]{1,0:T(8,128)S(1)} %get-tuple-element.44), channel_id=1, source_target_pairs={{0,16},{8,24},{16,0},{24,8},{1,17},{9,25},{17,1},{25,9},{2,18},{10... | collective-permute-start | bytes 602120 | tf_op jit(solution)/shard_map/ppermute | solution.py:349
  9.6 9.6 %collective-permute-start.5 = (f32[392,128]{1,0:T(8,128)S(1)}, f32[392,128]{1,0:T(8,128)S(1)}, u32[]{:S(2)}, u32[]{:S(2)}) collective-permute-start(f32[392,128]{1,0:T(8,128)S(1)} %get-tuple-element.45), channel_id=1, source_target_pairs={{0,24},{8,16},{16,8},{24,0},{1,25},{9,17},{17,9},{25,1},{2,26},{10... | collective-permute-start | bytes 602120 | tf_op jit(solution)/shard_map/ppermute | solution.py:349
  9.9 3.7 %collective-permute-start.1 = (f32[2,8,2,128]{3,2,1,0:T(2,128)S(1)}, f32[2,8,2,128]{3,2,1,0:T(2,128)S(1)}, u32[]{:S(2)}, u32[]{:S(2)}) collective-permute-start(f32[2,8,2,128]{3,2,1,0:T(2,128)S(1)} %pad_maximum_fusion.1), channel_id=1, source_target_pairs={{0,2},{1,3},{2,0},{3,1},{4,6},{5,7},{6,4},{7,5},{8,10},{9,11},{10,... | collective-permute-start | bytes 49160 | tf_op jit(solution)/shard_map/ppermute | solution.py:349
  13.6 5.1 %collective-permute-start.2 = (f32[4,8,2,128]{3,2,1,0:T(2,128)S(1)}, f32[4,8,2,128]{3,2,1,0:T(2,128)S(1)}, u32[]{:S(2)}, u32[]{:S(2)}) collective-permute-start(f32[4,8,2,128]{3,2,1,0:T(2,128)S(1)} %pad_maximum_fusion.shocks_ref), channel_id=1, source_target_pairs={{0,4},{1,5},{2,6},{3,7},{4,0},{5,1},{6,2},{7,3},{8,12},{9,13},{10,... | collective-permute-start | bytes 98312 | tf_op jit(solution)/shard_map/ppermute | solution.py:349
  41.5 4.4 %collective-permute-start.7 = (f32[128,128]{1,0:T(8,128)S(1)}, f32[128,128]{1,0:T(8,128)S(1)}, u32[]{:S(2)}, u32[]{:S(2)}) collective-permute-start(f32[128,128]{1,0:T(8,128)S(1)} %value.1.rest_0_), channel_id=1, source_target_pairs={{0,16},{8,24},{16,0},{24,8},{1,17},{9,25},{17,1},{25,9},{2,18},{10... | collective-permute-start | bytes 196616 | tf_op jit(solution)/shard_map/ppermute | solution.py:349
  43.1 5.4 %collective-permute-start.6 = (f32[128,128]{1,0:T(8,128)S(1)}, f32[128,128]{1,0:T(8,128)S(1)}, u32[]{:S(2)}, u32[]{:S(2)}) collective-permute-start(f32[128,128]{1,0:T(8,128)S(1)} %value.1.rest_0_), channel_id=1, source_target_pairs={{0,8},{8,0},{16,24},{24,16},{1,9},{9,1},{17,25},{25,17},{2,10},{10... | collective-permute-start | bytes 196616 | tf_op jit(solution)/shard_map/ppermute | solution.py:349
  45.9 2.8 %collective-permute-start.8 = (f32[128,128]{1,0:T(8,128)S(1)}, f32[128,128]{1,0:T(8,128)S(1)}, u32[]{:S(2)}, u32[]{:S(2)}) collective-permute-start(f32[128,128]{1,0:T(8,128)S(1)} %collective-permute-done.7.rest_0_), channel_id=1, source_target_pairs={{0,8},{8,0},{16,24},{24,16},{1,9},{9,1},{17,25},{25,17},{2,10},{10... | collective-permute-start | bytes 196616 | tf_op jit(solution)/shard_map/ppermute | solution.py:349
